TPU v7x, 256 devices: a whole 4x4x8 slice. The times are simulated.
256 devices in a mesh: dp: 64 (over z, x, core), feat: 4 (over y).
Axes of the slice: x: 4, y: 4, z: 8, core: 2. Of those that a mesh axis runs over, the one named last changes fastest.
Arguments:
- embeddings: bfloat16 [262144, 2048], P('dp', 'feat'), may hold values from -6 to 6
- sample_owner: int32 [262144], P('dp'), may hold values from 0 to 1535
- lloyd_assign: int32 [2, 1536], P(None, 'dp'), may hold values from 0 to 1023
- init_centroids: float32 [1024, 2048], P('dp', 'feat'), may hold values from -6 to 6
Outputs:
- centroids: float32 [1024, 2048], P('dp', 'feat')
- spread: float32 [2, 1536], P(None, 'dp')
All inputs are finite; a program needn't handle non-finite values.
Results may differ from a plain program's by a relative error of at most 0.0003.
Values sent between devices are 32-bit elements; how exact they have to be, the bound alone decides.
A program may use at most 64 MiB of HBM per device.

v0:
```python
import math

import jax
import jax.numpy as jnp
from jax import lax
from jax.sharding import Mesh
from jax.sharding import PartitionSpec as P

D = 2048
DP = ("dp_0", "dp_1", "dp_2")


EPS = 1e-06


def cut_along(x, dim, peers):
    dims = x.shape
    tiles = x.reshape(*dims[:dim], peers, dims[dim] // peers, *dims[dim + 1 :])
    return jnp.moveaxis(tiles, dim, 0)


def sum_at_owner(x, axis, dim):
    tiles = cut_along(x, dim, lax.axis_size(axis))
    arrived = lax.all_to_all(tiles, axis, split_axis=0, concat_axis=0, tiled=True)
    return arrived.sum(axis=0)


def sum_in_two_steps(x, axes, dim):
    far, near = axes
    tiles = cut_along(x, dim, lax.axis_size(far))
    nearer = sum_at_owner(tiles, near, dim + 1)
    arrived = lax.all_to_all(nearer, far, split_axis=0, concat_axis=0, tiled=True)
    return arrived.sum(axis=0)


def side_by_side(arrays, axis, dim, along):
    widths = [math.prod(a.shape[along:]) for a in arrays]
    both = jnp.concatenate(
        [a.reshape(*a.shape[:along], w) for a, w in zip(arrays, widths)], axis=along
    )
    whole = sum_in_two_steps(both, axis, dim)
    tiles = jnp.split(whole, [sum(widths[:k]) for k in range(1, len(widths))], axis=along)
    return tuple((b.reshape(*whole.shape[:along], *a.shape[along:]) for a, b in zip(arrays, tiles)))


def copy_for_each(x, axis):
    copies = jnp.broadcast_to(x, (lax.axis_size(axis), *x.shape))
    return lax.all_to_all(copies, axis, split_axis=0, concat_axis=0, tiled=True)


def of_everyone(x, axis):
    everything = copy_for_each(x, axis)
    return jnp.sum(everything, axis=0)


def in_order(tiles, dim):
    dims = list(tiles.shape[1:])
    dims[dim] *= tiles.shape[0]
    return jnp.moveaxis(tiles, 0, dim).reshape(dims)


def gather_axes(x, axes, dim):
    far, near = axes
    first = copy_for_each(x, far)
    tiles = jnp.swapaxes(copy_for_each(first, near), 0, 1)
    return in_order(tiles.reshape(-1, *x.shape), dim)


def side_by_side_2(arrays, axis, dim, along):
    columns = [a.reshape(*a.shape[:along], -1) for a in arrays]
    both = jnp.concatenate(columns, axis=along)
    whole, at, finished = (gather_axes(both, axis, dim), 0, [])
    for a, column in zip(arrays, columns):
        share = whole[..., at : at + column.shape[along]]
        finished.append(share.reshape(*share.shape[:along], *a.shape[along:]))
        at += column.shape[along]
    return tuple(finished)


def gathered_total(x, axis):
    return lax.all_gather(x, axis).sum(0)


def per_device(embeddings, sample_owner, lloyd_assign, init_centroids):
    n_parts = lax.axis_size(DP)
    c_local = lloyd_assign.shape[1]
    k_local = init_centroids.shape[0]
    cands = c_local * n_parts
    clusters = k_local * n_parts
    highest = lax.Precision.HIGHEST
    count_all = jax.ops.segment_sum(jnp.ones(sample_owner.shape, jnp.float32), sample_owner, cands)
    labels = lax.iota(jnp.int32, cands)
    onehot = (sample_owner[:, None] == labels[None, :]).astype(jnp.bfloat16)
    sums, counts = side_by_side(
        (
            lax.dot_general(
                onehot, embeddings, (((0,), (0,)), ((), ())), preferred_element_type=jnp.float32
            ),
            count_all,
        ),
        (("dp_0", "dp_1"), "dp_2"),
        0,
        1,
    )
    squares = of_everyone(jnp.sum(sums * sums, axis=1), "feat")
    means = sums * lax.rsqrt(squares / D + EPS)[:, None]
    start_row = lax.axis_index(DP) * k_local
    assign_rows = jnp.transpose(lloyd_assign).astype(jnp.float32)
    means_all, counts_all, assign_all = side_by_side_2(
        (means, counts, assign_rows), (("dp_0", "dp_1"), "dp_2"), 0, 1
    )
    weighted_all = counts_all[:, None] * means_all
    label_grid = lax.iota(jnp.int32, clusters).astype(jnp.float32)
    prev_own = init_centroids
    spreads = []
    for step in range(2):
        assign = lloyd_assign[step]
        labels_all = assign_all[:, step]
        onehot_all = (labels_all[:, None] == label_grid[None, :]).astype(jnp.float32)
        total = lax.dot_general(
            onehot_all, weighted_all, (((0,), (0,)), ((), ())), precision=highest
        )
        weight = jnp.dot(counts_all, onehot_all, precision=highest)
        length = of_everyone(jnp.sum(total * total, axis=1), "feat")
        table = total * lax.rsqrt(length / D + EPS)[:, None]
        fresh_own = lax.dynamic_slice_in_dim(table, start_row, k_local, 0)
        weight_own = lax.dynamic_slice_in_dim(weight, start_row, k_local, 0)
        prev_own = jnp.where(weight_own[:, None] > 0, fresh_own, prev_own)
        diff = means - jnp.take(table, assign, axis=0)
        distance = gathered_total(jnp.sum(diff * diff, axis=1), "feat")
        spreads.append(distance / D)
    return (prev_own, jnp.stack(spreads))


def solution(mesh):
    split = Mesh(
        mesh.devices.reshape(8, 4, 2, mesh.shape["feat"]), ("dp_0", "dp_1", "dp_2", "feat")
    )
    return jax.shard_map(
        per_device,
        mesh=split,
        in_specs=(P(DP, "feat"), P(DP), P(None, DP), P(DP, "feat")),
        out_specs=(P(DP, "feat"), P(None, DP)),
        check_vma=False,
    )
```

profile of v0, /device:TPU:1, one launch (start us, length us, event | category | flops | bytes accessed | tf_op | source)
XLA Modules:
  0.0 229.0 jit_solution(2640890893048847876)
XLA Ops:
  0.6 22.9 %scatter_custom_fusion = f32[1536]{0:T(1024)S(1)} fusion(s32[4096]{0:T(1024)} %param.7, f32[4096]{0:T(1024)S(1)} %broadcast.96, f32[]{:T(128)} %constant.22.clone.1), kind=kCustom, calls=%fused_computation.48 | custom fusion | flops 4096 | bytes 6656 | tf_op jit(solution)/shard_map/scatter-add | solution.py:91
  23.5 0.1 concatenate.12
  23.6 0.5 copy.18
  24.1 9.8 %fusion = f32[1536,512]{1,0:T(8,128)S(1)} fusion(bf16[4096,512]{1,0:T(8,128)(2,1)} %param.6, s32[4096]{0:T(1024)} %param.7), kind=kOutput, calls=%fused_computation.4 | convolution fusion | flops 6448742400 | bytes 7356416 | tf_op jit(solution)/shard_map/dot_general | solution.py:96
  33.8 0.4 maximum_bitcast_fusion
  34.2 10.7 %all_to_all.39 = f32[2,32,24,513]{3,2,1,0:T(8,128)} all-to-all(f32[2,32,24,513]{3,2,1,0:T(8,128)S(1)} %maximum_bitcast_fusion), channel_id=1, replica_groups=mesh['dp_0'=8,'dp_1'=4,'dp_2'=2,'feat'=4] {'dp_2'}, dimensions={0} | all-to-all | bytes 6303744 | tf_op jit(solution)/shard_map/all_to_all | solution.py:24
  44.9 2.6 %reduce_sum.108 = f32[32,24,513]{2,1,0:T(8,128)S(1)} reduce(f32[2,32,24,513]{3,2,1,0:T(8,128)} %all_to_all.39, f32[]{:T(128)} %constant.22.clone.1), dimensions={0}, to_apply=%region_1.0 | reduce | flops 393984 | bytes 4727812 | tf_op jit(solution)/shard_map/reduce_sum | solution.py:25
  47.5 0.0 copy-start.1
  47.5 55.7 %all_to_all.40 = f32[32,24,513]{2,1,0:T(8,128)} all-to-all(f32[32,24,513]{2,1,0:T(8,128)S(1)} %reduce_sum.108), channel_id=1, replica_groups=mesh['dp_0'=8,'dp_1'=4,'dp_2'=2,'feat'=4] {'dp_0','dp_1'}, dimensions={0} | all-to-all | bytes 3151872 | tf_op jit(solution)/shard_map/all_to_all | solution.py:32
  103.2 1.7 reduce_sum.109
  104.8 0.1 multiply_reduce_fusion.2
  105.0 0.6 broadcast_in_dim.58
  105.5 4.2 %all-to-all-start.2 = ((f32[4,1,24]{2,1,0:T(1,128)}), f32[4,1,24]{2,1,0:T(1,128)S(1)}, u32[]{:S(2)}, u32[]{:S(2)}) async-start(f32[4,1,24]{2,1,0:T(1,128)} %broadcast_in_dim.58), calls=%async_computation.2 | async-start | bytes 4096 | tf_op jit(solution)/shard_map/all_to_all | solution.py:48
  109.7 0.1 copy.20
  109.8 3.9 %all-to-all-done.2 = f32[4,1,24]{2,1,0:T(1,128)S(1)} async-done(((f32[4,1,24]{2,1,0:T(1,128)}), f32[4,1,24]{2,1,0:T(1,128)S(1)}, u32[]{:S(2)}, u32[]{:S(2)}) %all-to-all-start.2) | async-done | bytes 416 | tf_op jit(solution)/shard_map/all_to_all | solution.py:48
  113.8 0.1 slice_multiply_fusion.3
  113.8 0.1 pad_maximum_fusion
  113.9 1.4 broadcast_in_dim.59
  115.3 6.0 %all-to-all-start.3 = ((f32[32,24,515]{2,1,0:T(8,128)}), f32[32,24,515]{2,1,0:T(8,128)S(1)}, u32[]{:S(2)}, u32[]{:S(2)}) async-start(f32[32,24,515]{2,1,0:T(8,128)} %broadcast_in_dim.59), calls=%async_computation.3 | async-start | bytes 3932160 | tf_op jit(solution)/shard_map/all_to_all | solution.py:48
  121.3 0.6 dynamic-slice
  122.6 41.2 %all-to-all-done.3 = f32[32,24,515]{2,1,0:T(8,128)S(1)} async-done(((f32[32,24,515]{2,1,0:T(8,128)}), f32[32,24,515]{2,1,0:T(8,128)S(1)}, u32[]{:S(2)}, u32[]{:S(2)}) %all-to-all-start.3) | async-done | bytes 1582112 | tf_op jit(solution)/shard_map/all_to_all | solution.py:48
  163.8 0.3 broadcast_in_dim.60
  164.0 12.4 %all_to_all.38 = f32[2,32,24,515]{3,2,1,0:T(8,128)S(1)} all-to-all(f32[2,32,24,515]{3,2,1,0:T(8,128)S(1)} %broadcast_in_dim.60), channel_id=1, replica_groups=mesh['dp_0'=8,'dp_1'=4,'dp_2'=2,'feat'=4] {'dp_2'}, dimensions={0} | all-to-all | bytes 6328320 | tf_op jit(solution)/shard_map/all_to_all | solution.py:48
  176.4 0.3 copy.21
  176.7 1.1 slice_reduce_fusion.1
  177.8 7.2 %multiply_reduce_fusion.1 = (f32[1024]{0:T(1024)S(1)}, f32[1024,512]{1,0:T(8,128)}) fusion(f32[1536,515]{1,0:T(8,128)S(1)} %bitcast.25, f32[1536]{0:T(1024)S(1)} %get-tuple-element.5, f32[1024]{0:T(1024)S(1)} %iota_convert_fusion, f32[1536]{0:T(1024)S(1)} %get-tuple-element.3), kind=kOutput, calls=%fused_computation.25 | convolution fusion | flops 9667083264 | bytes 5267456 | tf_op jit(solution)/shard_map/dot_general | solution.py:120
  185.1 1.9 fusion.8
  187.0 1.9 fusion.4
  188.9 7.5 %multiply_reduce_fusion = (f32[1024]{0:T(1024)S(1)}, f32[1024,512]{1,0:T(8,128)}) fusion(f32[1536,515]{1,0:T(8,128)S(1)} %bitcast.26, f32[1536]{0:T(1024)S(1)} %get-tuple-element.5, f32[1024]{0:T(1024)S(1)} %iota_convert_fusion, f32[1536]{0:T(1024)S(1)} %get-tuple-element.4), kind=kOutput, calls=%fused_computation.24 | convolution fusion | flops 9667083264 | bytes 5267456 | tf_op jit(solution)/shard_map/dot_general | solution.py:120
  196.4 0.6 broadcast_in_dim.62
  197.0 3.3 %all-to-all-start.5 = ((f32[4,1,1024]{2,1,0:T(1,128)}), f32[4,1,1024]{2,1,0:T(1,128)S(1)}, u32[]{:S(2)}, u32[]{:S(2)}) async-start(f32[4,1,1024]{2,1,0:T(1,128)} %broadcast_in_dim.62), calls=%async_computation.5 | async-start | bytes 32768 | tf_op jit(solution)/shard_map/all_to_all | solution.py:48
  200.3 0.1 dynamic-slice_compare_fusion
  200.4 4.1 %all-to-all-done.5 = f32[4,1,1024]{2,1,0:T(1,128)S(1)} async-done(((f32[4,1,1024]{2,1,0:T(1,128)}), f32[4,1,1024]{2,1,0:T(1,128)S(1)}, u32[]{:S(2)}, u32[]{:S(2)}) %all-to-all-start.5) | async-done | bytes 16416 | tf_op jit(solution)/shard_map/all_to_all | solution.py:48
  204.5 0.6 broadcast_in_dim.64
  205.1 3.3 %all-to-all-start.6 = ((f32[4,1,1024]{2,1,0:T(1,128)}), f32[4,1,1024]{2,1,0:T(1,128)S(1)}, u32[]{:S(2)}, u32[]{:S(2)}) async-start(f32[4,1,1024]{2,1,0:T(1,128)} %broadcast_in_dim.64), calls=%async_computation.6 | async-start | bytes 32768 | tf_op jit(solution)/shard_map/all_to_all | solution.py:48
  208.4 4.1 %all-to-all-done.6 = f32[4,1,1024]{2,1,0:T(1,128)S(1)} async-done(((f32[4,1,1024]{2,1,0:T(1,128)}), f32[4,1,1024]{2,1,0:T(1,128)S(1)}, u32[]{:S(2)}, u32[]{:S(2)}) %all-to-all-start.6) | async-done | bytes 16416 | tf_op jit(solution)/shard_map/all_to_all | solution.py:48
  212.5 0.0 copy-start
  212.6 3.9 %broadcast_multiply_fusion = (f32[1024,512]{1,0:T(8,128)S(1)}, f32[1024,512]{1,0:T(8,128)}) fusion(f32[1024,512]{1,0:T(8,128)} %get-tuple-element.17, f32[1024]{0:T(1024)S(1)} %add_rsqrt_fusion, f32[1024,512]{1,0:T(8,128)} %get-tuple-element.19, f32[1024]{0:T(1024)S(1)} %add_rsqrt_fusion.1), kind=kLoop, calls=%fused_computation.28 | loop fusion | flops 1048576 | bytes 8396800 | tf_op jit(solution)/shard_map/mul | solution.py:125
  216.4 2.2 gather_fusion.1
  218.6 0.6 gather_fusion
  219.2 0.2 fusion.23
  219.4 0.2 dynamic-update-slice
  219.7 0.2 dynamic-update-slice.1
  219.9 6.8 %all-reduce.2 = (f32[96]{0:T(128)S(1)}, f32[96]{0:T(128)S(1)}) all-reduce(f32[96]{0:T(128)S(1)} %dynamic-update-slice.1, f32[96]{0:T(128)S(1)} %dynamic-update-slice), channel_id=3, replica_groups=mesh['dp_0'=8,'dp_1'=4,'dp_2'=2,'feat'=4] {'feat'}, use_global_device_ids=true, to_apply=%add.1 | all-reduce | flops 192 | bytes 1536
  226.7 0.1 reshape.96
  226.9 0.1 reshape.95
  227.0 0.6 pad_maximum_fusion.1
  227.5 1.4 select_select_fusion
  (23 shorter events, 0.2 us)
Async XLA Ops:
  47.5 62.2 %copy-start.1 = (s32[2,24]{1,0:T(2,128)S(1)}, s32[2,24]{1,0:T(2,128)}, u32[]{:S(2)}) copy-start(s32[2,24]{1,0:T(2,128)} %param.8) | copy-start | bytes 580
  104.9 16.4 %copy-start.2 = (u32[256]{0:T(256)S(1)}, u32[256]{0:T(256)}, u32[]{:S(2)}) copy-start(u32[256]{0:T(256)} %constant.56) | copy-start | bytes 3076
  105.5 8.2 %all-to-all-start.2 = ((f32[4,1,24]{2,1,0:T(1,128)}), f32[4,1,24]{2,1,0:T(1,128)S(1)}, u32[]{:S(2)}, u32[]{:S(2)}) async-start(f32[4,1,24]{2,1,0:T(1,128)} %broadcast_in_dim.58), calls=%async_computation.2 | async-start | bytes 4096 | tf_op jit(solution)/shard_map/all_to_all | solution.py:48
  115.3 48.4 %all-to-all-start.3 = ((f32[32,24,515]{2,1,0:T(8,128)}), f32[32,24,515]{2,1,0:T(8,128)S(1)}, u32[]{:S(2)}, u32[]{:S(2)}) async-start(f32[32,24,515]{2,1,0:T(8,128)} %broadcast_in_dim.59), calls=%async_computation.3 | async-start | bytes 3932160 | tf_op jit(solution)/shard_map/all_to_all | solution.py:48
  197.0 7.4 %all-to-all-start.5 = ((f32[4,1,1024]{2,1,0:T(1,128)}), f32[4,1,1024]{2,1,0:T(1,128)S(1)}, u32[]{:S(2)}, u32[]{:S(2)}) async-start(f32[4,1,1024]{2,1,0:T(1,128)} %broadcast_in_dim.62), calls=%async_computation.5 | async-start | bytes 32768 | tf_op jit(solution)/shard_map/all_to_all | solution.py:48
  205.1 7.4 %all-to-all-start.6 = ((f32[4,1,1024]{2,1,0:T(1,128)}), f32[4,1,1024]{2,1,0:T(1,128)S(1)}, u32[]{:S(2)}, u32[]{:S(2)}) async-start(f32[4,1,1024]{2,1,0:T(1,128)} %broadcast_in_dim.64), calls=%async_computation.6 | async-start | bytes 32768 | tf_op jit(solution)/shard_map/all_to_all | solution.py:48
  212.5 15.0 %copy-start = (f32[16,512]{1,0:T(8,128)S(1)}, f32[16,512]{1,0:T(8,128)}, u32[]{:S(2)}) copy-start(f32[16,512]{1,0:T(8,128)} %param.9) | copy-start | bytes 98308
where the time goes:
time: 233 us; the launch traced here: 229 us
  blocking collectives  85.6 us (37%)
  waiting for transfers between devices  53.3 us (23%)
  other arithmetic  34.1 us (15%)
  matrix products  28.3 us (12%)
  starting transfers between devices  16.6 us (7%)
  local copies, waits for them, and re-layouts  9.52 us (4%)
    all_to_all x1, blocking collectives, sum_in_two_steps(): lax.all_to_all(nearer, far, split_axis=0, concat_axis=0, tiled=True)  55.7 us
    all_to_all x4, waiting for transfers between devices, copy_for_each(): return lax.all_to_all(copies, axis, split_axis=0, concat_axis=0, tiled=True)  53.3 us
    scatter-add x1, other arithmetic, per_device(): jax.ops.segment_sum(jnp.ones(sample_owner.shape, jnp.float32), sample_own...  22.9 us
    all_to_all x4, starting transfers between devices, copy_for_each(): return lax.all_to_all(copies, axis, split_axis=0, concat_axis=0, tiled=True)  16.6 us
    dot_general x2, matrix products, per_device(): lax.dot_general(onehot_all, weighted_all, (((0,), (0,)), ((), ())), preci...  14.7 us
    all_to_all x1, blocking collectives, copy_for_each(): return lax.all_to_all(copies, axis, split_axis=0, concat_axis=0, tiled=True)  12.4 us
    all_to_all x1, blocking collectives, sum_at_owner(): lax.all_to_all(tiles, axis, split_axis=0, concat_axis=0, tiled=True)  10.7 us
    dot_general x1, matrix products, per_device(): lax.dot_general(onehot, embeddings, (((0,), (0,)), ((), ())), preferred_e...  9.76 us
  transfers between devices with their start and end apart: 4, of which 4 were waited for; matrix products, arithmetic and copies ran while one was open for 0% of the time, Pallas kernels for 0%

commit v1 on v0

v1 whole, which is shorter than its diff:
```python
import jax
import jax.numpy as jnp
from jax import lax
from jax.experimental import pallas as pl
from jax.experimental.pallas import tpu as pltpu
from jax.sharding import PartitionSpec as P

EPS = 1e-06
MESH = pl.DeviceIdType.MESH

NZ, NX, NC, NY = 8, 4, 2, 4
OWN = 24
ROWS = NX * OWN
BLOCKS = NZ * NC
HEAD = 40
TAIL = ROWS - HEAD
CUT = 64
LANE = 128
ORDER = ((4, 3), (-3, 2), (-2, 1), (-1, 0))


def position(owner):
    slab = lax.shift_right_logical(owner * 21846, 22)
    left = owner - slab * (NX * NC * OWN)
    column = lax.shift_right_logical(left * 1366, 16)
    inner = left - column * (NC * OWN)
    core = jnp.where(inner >= OWN, 1, 0)
    block = slab * NC + core
    return block, column * OWN + inner - core * OWN


def as_rows(columns, pad_ref):
    pad_ref[...] = jnp.zeros_like(pad_ref)
    lane = lax.broadcasted_iota(jnp.int32, (ROWS, LANE), 1)
    filled = jnp.zeros((ROWS, LANE), jnp.float32)
    for j, column in enumerate(columns):
        filled = jnp.where(lane == j, column, filled)
    pad_ref[0:ROWS, :] = filled
    return jnp.transpose(pad_ref[...])[0:8, :]


def as_columns(tile):
    return jnp.transpose(tile)


def kernel(
    depth, width, features,
    owner_ref, assign_ref, init_ref, emb_hbm,
    cent_ref, spread_ref,
    emb, part, other, other_in, xin, zr, zl, qr, ql, hx,
    prow, info, info_x, group, info_z, counts, match, weight, pad, wrows,
    table, sq_own, sq_in, scale, scale2, scaled, final_own, final_in, sel, sel_in, lens,
    load_sem, send_sem, recv_sem,
):
    dp, y = lax.axis_index("dp"), lax.axis_index("feat")
    z, x, c = lax.div(dp, NX * NC), lax.rem(lax.div(dp, NC), NX), lax.rem(dp, NC)

    def zat(d):
        return lax.rem(z + d + NZ, NZ)

    def xat(d):
        return lax.rem(x + d + NX, NX)

    def device(dz=0, dx=0, dc=0, dy=0):
        return (zat(dz) * (NX * NC) + xat(dx) * NC + lax.rem(c + dc, NC), lax.rem(y + dy, NY))

    used = [0]
    sent = []

    def copy_at(slot, src, dst, to):
        return pltpu.make_async_remote_copy(
            src_ref=src, dst_ref=dst, send_sem=send_sem.at[slot], recv_sem=recv_sem.at[slot],
            device_id=to, device_id_type=MESH,
        )

    def go(src, dst, to):
        copy = copy_at(used[0], src, dst, to)
        used[0] += 1
        copy.start()
        sent.append(copy.wait_send)
        return copy

    def go_all(first, last, make):
        base = used[0]
        used[0] += last - first

        def at(j):
            src, dst, to = make(j)
            return copy_at(base + j - first, src, dst, to)

        def run(act):
            def step(j, carry):
                act(at(j))
                return carry
            lax.fori_loop(first, last, step, 0)

        run(lambda copy: copy.start())
        sent.append(lambda: run(lambda copy: copy.wait_send()))
        return lambda: run(lambda copy: copy.wait_recv())

    chunks = emb.shape[0] // depth
    loads = [
        pltpu.make_async_copy(
            emb_hbm.at[pl.ds(k * depth, depth)], emb.at[pl.ds(k * depth, depth)], load_sem.at[k]
        )
        for k in range(chunks)
    ]
    for load in loads:
        load.start()

    barrier = pltpu.get_barrier_semaphore()

    def greet(first, last, to):
        def step(j, carry):
            pl.semaphore_signal(barrier, inc=1, device_id=to(j), device_id_type=MESH)
            return carry
        lax.fori_loop(first, last, step, 0)

    greet(1, 8, lambda j: device(dx=lax.div(j, 2), dc=lax.rem(j, 2)))
    greet(0, 12, lambda j: device(dx=lax.div(j, 3), dy=lax.rem(j, 3) + 1))
    greet(2, 16, lambda j: device(dz=lax.div(j, 2), dc=lax.rem(j, 2)))

    block, place = position(owner_ref[...])
    prow[...] = block * ROWS + place
    samples = owner_ref.shape[1]
    high = lax.broadcasted_iota(jnp.int32, (BLOCKS, samples), 0) == block
    low = lax.broadcasted_iota(jnp.int32, (LANE, samples), 0) == place
    info[0:BLOCKS, :] = lax.dot_general(
        jnp.where(high, 1.0, 0.0).astype(jnp.bfloat16),
        jnp.where(low, 1.0, 0.0).astype(jnp.bfloat16),
        (((1,), (1,)), ((), ())), preferred_element_type=jnp.float32,
    )
    placed = pltpu.roll(assign_ref[...], x * OWN, 1)
    info[BLOCKS : BLOCKS + 8, :] = jnp.where(c == 0, placed, pltpu.roll(placed, 2, 0))
    part[...] = jnp.zeros_like(part)
    other[...] = jnp.zeros_like(other)

    pl.semaphore_wait(barrier, 7 + 12 + 14)

    arrived = go_all(
        1, 8, lambda j: (info, info_x.at[j], device(dx=lax.div(j, 2), dc=lax.rem(j, 2)))
    )
    info_x[0] = info[...]

    def sums(slabs, core, into, waits=()):
        bases = [slab * (NC * ROWS) + core * ROWS for slab in slabs]
        row = lax.broadcasted_iota(jnp.int32, (ROWS, depth), 0)

        def step(k):
            at = pl.ds(pl.multiple_of(k * depth, depth), depth)
            p = prow[:, at]
            hot = jnp.concatenate(
                [jnp.where(row == p - base, 1.0, 0.0).astype(jnp.bfloat16) for base in bases], 0
            )
            got = jnp.dot(hot, emb[at, :], preferred_element_type=jnp.float32)
            for j, ref in enumerate(into):
                for b in range(NX):
                    ref[b] += got[j * ROWS : (j + 1) * ROWS, b * LANE : (b + 1) * LANE]

        if waits:
            for k in range(chunks):
                waits[k].wait()
                step(k)
        else:
            lax.fori_loop(0, chunks, lambda k, carry: (step(k), carry)[1], 0)

    cross = {}

    def work(g):
        slabs = [zat(d) for d in ORDER[g]]
        sums(slabs, 1 - c, [other.at[g, 0], other.at[g, 1]], loads if g == 0 else ())
        cross[g] = go(other.at[g], other_in.at[g], device(dc=1))
        sums(slabs, c, [part.at[slab] for slab in slabs])

    def meet(g):
        cross[g].wait_recv()
        for j, d in enumerate(ORDER[g]):
            part[zat(d)] += other_in[g, j]

    tail = pl.ds(HEAD, TAIL)
    xs = {}

    def x_start(g):
        first, second = (zat(d) for d in ORDER[g])
        right, left = device(dx=1), device(dx=-1)
        xs[g, 0] = go(part.at[first, xat(2), tail], xin.at[g, 0], right)
        xs[g, 3] = go(part.at[second, xat(2), tail], xin.at[g, 3], left)
        xs[g, 1] = go(part.at[second, xat(1), tail], xin.at[g, 1], right)
        xs[g, 4] = go(part.at[first, xat(-1), tail], xin.at[g, 4], left)

    def x_mid(g):
        first, second = (zat(d) for d in ORDER[g])
        xs[g, 0].wait_recv()
        part[first, xat(1), HEAD:ROWS] += xin[g, 0]
        xs[g, 2] = go(part.at[first, xat(1), tail], xin.at[g, 2], device(dx=1))
        xs[g, 3].wait_recv()
        part[second, xat(-1), HEAD:ROWS] += xin[g, 3]
        xs[g, 5] = go(part.at[second, xat(-1), tail], xin.at[g, 5], device(dx=-1))

    def x_end(g):
        first, second = (zat(d) for d in ORDER[g])
        xs[g, 4].wait_recv()
        xs[g, 2].wait_recv()
        part[first, x, HEAD:ROWS] += xin[g, 4] + xin[g, 2]
        xs[g, 1].wait_recv()
        xs[g, 5].wait_recv()
        part[second, x, HEAD:ROWS] += xin[g, 1] + xin[g, 5]

    head = pl.ds(0, HEAD)
    zs = {}

    def z_head(h, way):
        slab = zat((4 - h) * way)
        into, half = (zr, 0) if way > 0 else (zl, 2)
        if h == 0:
            at = pl.ds(half, 2)
            zs[h, way] = go(part.at[slab, at, head], into.at[0, at], device(dz=way))
            return
        zs[h - 1, way].wait_recv()
        if h == 1:
            part[slab, half : half + 2, 0:HEAD] += into[0, half : half + 2]
        else:
            part[slab, :, 0:HEAD] += into[h - 1]
        zs[h, way] = go(part.at[slab, :, head], into.at[h], device(dz=way))

    def z_head_end():
        zs[3, 1].wait_recv()
        zs[3, -1].wait_recv()
        part[z, :, 0:HEAD] += zr[3] + zl[3]

    ts = {}

    def z_tail(h, way):
        slab = zat((4 - h) * way)
        into, start, size = (qr, HEAD, CUT - HEAD) if way > 0 else (ql, CUT, ROWS - CUT)
        if h == 0:
            ts[h, way] = go(
                part.at[slab, x, pl.ds(start, size)], into.at[0, pl.ds(0, size)], device(dz=way)
            )
            return
        ts[h - 1, way].wait_recv()
        if h == 1:
            part[slab, x, start : start + size] += into[0, 0:size]
        else:
            part[slab, x, HEAD:ROWS] += into[h - 1]
        ts[h, way] = go(part.at[slab, x, tail], into.at[h], device(dz=way))

    def z_tail_end():
        ts[3, 1].wait_recv()
        ts[3, -1].wait_recv()
        part[z, x, HEAD:ROWS] += qr[3] + ql[3]

    work(0)
    meet(0)
    z_head(0, 1)
    z_head(0, -1)
    x_start(0)

    arrived()
    whole = info_x[0]
    for j in range(1, NX * NC):
        whole = whole + info_x[j]
    group[...] = whole
    info_z[z] = whole
    arrived_z = go_all(1, NZ, lambda j: (group, info_z.at[z], device(dz=j)))

    work(1)
    meet(1)
    z_head(1, 1)
    z_head(1, -1)
    x_mid(0)
    x_start(1)

    work(2)
    meet(2)
    z_head(2, 1)
    z_head(2, -1)
    x_mid(1)
    x_start(2)
    x_end(0)
    z_tail(0, 1)
    z_tail(0, -1)

    work(3)
    meet(3)
    z_head(3, 1)
    z_head(3, -1)
    x_mid(2)
    x_start(3)
    x_end(1)
    z_tail(1, 1)
    z_tail(1, -1)
    x_mid(3)
    x_end(2)
    z_tail(2, 1)
    z_tail(2, -1)
    z_head_end()
    hop = go(part.at[z, xat(2), head], hx.at[0], device(dx=1))
    back = go(part.at[z, xat(-1), head], hx.at[1], device(dx=-1))
    x_end(3)
    z_tail(3, 1)
    z_tail(3, -1)
    hop.wait_recv()
    part[z, xat(1), 0:HEAD] += hx[0]
    last = go(part.at[z, xat(1), head], hx.at[2], device(dx=1))
    z_tail_end()
    back.wait_recv()
    last.wait_recv()
    part[z, x, 0:HEAD] += hx[1] + hx[2]

    own = part[z, x]
    mine = z * NC + c
    table[mine] = own

    rings = {}

    def blk(dz):
        return zat(dz) * NC + c

    def z_share(h, way):
        at = blk(-h * way)
        if h == 3:
            rows = pl.ds(0, ROWS // 2) if way > 0 else pl.ds(ROWS // 2, ROWS // 2)
        else:
            rows = pl.ds(0, ROWS)
        rings[h, way] = go(table.at[at, rows], table.at[at, rows], device(dz=way))

    pairs = []

    def core_share(dz):
        at = blk(dz)
        pairs.append(go(table.at[at], table.at[at], device(dc=1)))

    z_share(0, 1)
    z_share(0, -1)
    core_share(0)

    square = jnp.sum(own * own, axis=1, keepdims=True)
    sq_own[0] = as_rows([square], pad)[0:1, :]
    sq_arrived = go_all(
        1, NX * NY,
        lambda j: (sq_own.at[0], sq_in.at[j], device(dx=lax.div(j, NY), dy=lax.rem(j, NY))),
    )

    arrived_z()
    total = info_z[0, 0:BLOCKS]
    for j in range(1, NZ):
        total = total + info_z[j, 0:BLOCKS]
    counts[...] = total

    for way in (1, -1):
        rings[0, way].wait_recv()
        z_share(1, way)
    core_share(-1)
    core_share(1)

    keys_all = group[BLOCKS : BLOCKS + 8, :]
    keys = as_columns(jnp.where(c == 0, keys_all, pltpu.roll(keys_all, 6, 0)))
    cents = NX * cent_ref.shape[0]
    r = lax.broadcasted_iota(jnp.int32, (cents, LANE), 0)
    per = cent_ref.shape[0]
    r = z * (cents * NC) + lax.div(r, per) * (per * NC) + c * per + lax.rem(r, per)
    cent_key = r.astype(jnp.float32)
    spread_key = [jnp.broadcast_to(keys[0:ROWS, t : t + 1], (ROWS, LANE)) for t in range(2)]
    parts = [
        (0, cents, cent_key, 0), (cents, cents, cent_key, 1),
        (2 * cents, ROWS, spread_key[0], 0), (2 * cents + ROWS, ROWS, spread_key[1], 1),
    ]
    weight[...] = jnp.zeros_like(weight)
    for b in range(BLOCKS):
        many = counts[b : b + 1, :]
        for at, n, key, t in parts:
            line = BLOCKS + 2 * (b % NC) + t
            same = jnp.where(key == info_z[b // NC, line : line + 1, :], 1.0, 0.0)
            match[at : at + n, b * LANE : (b + 1) * LANE] = same.astype(jnp.bfloat16)
            weight[at : at + n, :] += same * many
    summed = jnp.sum(weight[...], axis=1, keepdims=True)
    weight[...] = jnp.broadcast_to(summed, weight.shape)
    first_row = 2 * cents
    wrows[...] = as_rows(
        [summed[first_row : first_row + ROWS], summed[first_row + ROWS : first_row + 2 * ROWS]], pad
    )

    sq_arrived()
    square_row = sq_own[0]
    for j in range(1, NX * NY):
        square_row = square_row + sq_in[j]
    inverse = lax.rsqrt(square_row / features + EPS)
    scale[mine] = inverse
    scale_arrived = go_all(
        1, NZ * NC,
        lambda j: (scale.at[mine], scale.at[mine], device(dz=lax.div(j, NC), dc=lax.rem(j, NC))),
    )
    means = own * as_columns(jnp.broadcast_to(inverse, (8, LANE)))[0:ROWS, 0:1]

    for way in (1, -1):
        rings[1, way].wait_recv()
        z_share(2, way)
    core_share(-2)
    core_share(2)
    for way in (1, -1):
        rings[2, way].wait_recv()
        z_share(3, way)
    core_share(-3)
    core_share(3)

    scale_arrived()
    for b in range(BLOCKS):
        scale2[b : b + 1, :] = scale[b]
    factor = as_columns(counts[...] * scale2[...])
    rings[3, 1].wait_recv()
    rings[3, -1].wait_recv()
    core_share(4)
    for pair in pairs:
        pair.wait_recv()
    scaled[...] = jnp.zeros_like(scaled)
    for b in range(BLOCKS):
        rows = table[b] * factor[0:ROWS, b : b + 1]
        for piece in range(3):
            near = rows.astype(jnp.bfloat16)
            scaled[b * LANE : b * LANE + ROWS, piece * LANE : (piece + 1) * LANE] = near
            rows = rows - near.astype(jnp.float32)
    tot = jnp.dot(match[...], scaled[...], preferred_element_type=jnp.float32)
    tot = tot[:, 0:LANE] + (tot[:, LANE : 2 * LANE] + tot[:, 2 * LANE : 3 * LANE])

    columns = []
    for t in range(2):
        at = first_row + t * ROWS
        many = weight[at : at + ROWS, :]
        g = tot[at : at + ROWS] * jnp.where(many > 0, 1.0 / jnp.maximum(many, 1.0), 0.0)
        d = means - g
        for v in (d * d, d * g, g * g):
            columns.append(jnp.sum(v, axis=1, keepdims=True))
    chosen = jnp.where(weight[cents : 2 * cents, :] > 0, tot[cents : 2 * cents], tot[0:cents])
    sel[...] = chosen
    squares = jnp.sum(chosen * chosen, axis=1, keepdims=True)
    columns.append(jnp.concatenate([squares, jnp.zeros((ROWS - cents, 1), jnp.float32)], 0))
    final_own[...] = as_rows(columns, pad)
    final_arrived = go_all(
        1, NX * NY,
        lambda j: (final_own, final_in.at[j], device(dx=lax.div(j, NY), dy=lax.rem(j, NY))),
    )
    sel_arrived = go_all(
        1, NX, lambda j: (sel.at[pl.ds(xat(j) * per, per)], sel_in.at[x], device(dx=j))
    )
    here = pl.ds(pl.multiple_of(x * per, per), per)
    sel_in[x] = sel[here, :]

    final_arrived()
    last_sum = final_own[...]
    for j in range(1, NX * NY):
        last_sum = last_sum + final_in[j]
    for t in range(2):
        far, mixed, length = (last_sum[3 * t + j : 3 * t + j + 1] for j in range(3))
        many = wrows[t : t + 1, :]
        s = many * lax.rsqrt(many * many * (length / features) + EPS) - 1.0
        value = (far - 2.0 * s * mixed + s * s * length) / features
        value = pltpu.roll(jnp.broadcast_to(value, (8, LANE)), LANE - x * OWN, 1)
        spread_ref[t : t + 1, :] = value[0:1, 0:OWN]
    lens[...] = as_columns(last_sum)
    length = lens[here, 6:7]
    inverse = lax.rsqrt(length / features + EPS)
    first = weight[here, :]
    second = weight[pl.ds(pl.multiple_of(x * per + cents, per), per), :]
    keep = jnp.maximum(first, second) > 0
    sel_arrived()
    for b in range(NX):
        at = slice(b * LANE, (b + 1) * LANE)
        cent_ref[:, at] = jnp.where(keep, sel_in[b] * inverse, init_ref[:, at])

    for wait in sent:
        wait()


COPIES = 7 + 7 + 4 + 24 + 8 + 8 + 3 + 8 + 8 + 15 + 15 + 15 + 3


def per_device(features, embeddings, sample_owner, lloyd_assign, init_centroids):
    samples, width = embeddings.shape
    per = init_centroids.shape[0]
    depth = 1024
    f32, bf16 = jnp.float32, jnp.bfloat16
    vm = pltpu.VMEM
    cents = NX * per
    lines = 2 * (cents + ROWS)
    scratch = [
        vm((samples, width), bf16),
        vm((NZ, NX, ROWS, LANE), f32),
        vm((4, 2, NX, ROWS, LANE), f32),
        vm((4, 2, NX, ROWS, LANE), f32),
        vm((4, 6, TAIL, LANE), f32),
        vm((4, NX, HEAD, LANE), f32),
        vm((4, NX, HEAD, LANE), f32),
        vm((4, TAIL, LANE), f32),
        vm((4, TAIL, LANE), f32),
        vm((3, HEAD, LANE), f32),
        vm((1, samples), jnp.int32),
        vm((24, LANE), f32),
        vm((NX * NC, 24, LANE), f32),
        vm((24, LANE), f32),
        vm((NZ, 24, LANE), f32),
        vm((BLOCKS, LANE), f32),
        vm((lines, BLOCKS * LANE), bf16),
        vm((lines, LANE), f32),
        vm((LANE, LANE), f32),
        vm((8, LANE), f32),
        vm((BLOCKS, ROWS, LANE), f32),
        vm((1, 1, LANE), f32),
        vm((NX * NY, 1, LANE), f32),
        vm((BLOCKS, 1, LANE), f32),
        vm((BLOCKS, LANE), f32),
        vm((BLOCKS * LANE, 3 * LANE), bf16),
        vm((8, LANE), f32),
        vm((NX * NY, 8, LANE), f32),
        vm((cents, LANE), f32),
        vm((NX, per, LANE), f32),
        vm((LANE, 8), f32),
        pltpu.SemaphoreType.DMA((samples // depth,)),
        pltpu.SemaphoreType.DMA((COPIES,)),
        pltpu.SemaphoreType.DMA((COPIES,)),
    ]
    assign = jnp.pad(lloyd_assign.astype(f32), ((0, 6), (0, LANE - OWN)))
    in_vmem = pl.BlockSpec(memory_space=pltpu.VMEM)

    def body(*refs):
        kernel(depth, width, features, *refs)

    return pl.pallas_call(
        body,
        name="recluster",
        out_shape=(
            jax.ShapeDtypeStruct((per, width), f32),
            jax.ShapeDtypeStruct((2, OWN), f32),
        ),
        in_specs=[in_vmem, in_vmem, in_vmem, pl.BlockSpec(memory_space=pltpu.HBM)],
        out_specs=(in_vmem, in_vmem),
        scratch_shapes=scratch,
        compiler_params=pltpu.CompilerParams(
            collective_id=0, has_side_effects=True, vmem_limit_bytes=48 << 20
        ),
    )(sample_owner.reshape(1, samples), assign, init_centroids, embeddings)


def solution(mesh):
    def run(embeddings, sample_owner, lloyd_assign, init_centroids):
        features = embeddings.shape[1]
        return jax.shard_map(
            lambda *args: per_device(features, *args),
            mesh=mesh,
            in_specs=(P("dp", "feat"), P("dp"), P(None, "dp"), P("dp", "feat")),
            out_specs=(P("dp", "feat"), P(None, "dp")),
            check_vma=False,
        )(embeddings, sample_owner, lloyd_assign, init_centroids)

    return run
```

time: 233 us -> 66.4 us (0.28); the launches traced: 229 us -> 66.2 us
  blocking collectives: 85.6 us -> 0 us
  Pallas kernels: 0 us -> 60 us
  waiting for transfers between devices: 53.3 us -> 0 us
  other arithmetic: 34.1 us -> 0.68 us
  matrix products: 28.3 us -> 0 us
  starting transfers between devices: 16.6 us -> 0 us
  local copies, waits for them, and re-layouts: 9.52 us -> 4.85 us
    all_to_all x3 -> x0, blocking collectives: 78.8 us -> none  [the longest x1 55.7 us: sum_in_two_steps(): lax.all_to_all(nearer, far, split_axis=0, concat_axis=0, tiled=True)]
    pallas_call x0 -> x1, Pallas kernels: none -> 60 us  [per_device(): pl.pallas_call(body, name='recluster', out_shape=(jax.ShapeDtypeStruct((p...]
    all_to_all x4 -> x0, waiting for transfers between devices: 53.3 us -> none  [copy_for_each(): return lax.all_to_all(copies, axis, split_axis=0, concat_axis=0, tiled=True)]
    dot_general x5 -> x0, matrix products: 28.3 us -> none  [the longest x2 14.7 us: per_device(): lax.dot_general(onehot_all, weighted_all, (((0,), (0,)), ((), ())), preci...]
    scatter-add x1 -> x0, other arithmetic: 22.9 us -> none  [per_device(): jax.ops.segment_sum(jnp.ones(sample_owner.shape, jnp.float32), sample_own...]
    all_to_all x4 -> x0, starting transfers between devices: 16.6 us -> none  [copy_for_each(): return lax.all_to_all(copies, axis, split_axis=0, concat_axis=0, tiled=True)]
    unnamed x1 -> x0, blocking collectives: 6.85 us -> none
    reduce_sum x9 -> x0, other arithmetic: 4.68 us -> none  [the longest x1 2.6 us: sum_at_owner(): return arrived.sum(axis=0)]
  transfers between devices with their start and end apart: 4 -> 0, of which waited for: 4 -> 0; matrix products, arithmetic and copies ran while one was open for 0% -> 0% of each run, Pallas kernels for 0% -> 0%
where the time goes in v1:
time: 66.4 us; the launch traced here: 66.2 us
  Pallas kernels  60 us (90%)
  local copies, waits for them, and re-layouts  4.85 us (7%)
  other arithmetic  0.68 us (1%)
    pallas_call x1, Pallas kernels, per_device(): pl.pallas_call(body, name='recluster', out_shape=(jax.ShapeDtypeStruct((p...  60 us
    unnamed x8, local copies, waits for them, and re-layouts  4.84 us

profile of v1, /device:TPU:1, one launch (start us, length us, event | category | flops | bytes accessed | tf_op | source)
XLA Modules:
  0.0 66.2 jit_solution(15530062345530435880)
XLA Ops:
  0.6 0.7 %convert_element_type.5 = f32[2,24]{1,0:T(2,128)S(1)} convert(s32[2,24]{1,0:T(2,128)} %param.6) | non-fusion elementwise | flops 48 | bytes 384 | tf_op jit(solution)/shard_map/convert_element_type | solution.py:522
  1.3 0.0 copy-start
  1.3 2.2 %copy-done = bf16[4096,512]{1,0:T(8,128)(2,1)S(1)} copy-done((bf16[4096,512]{1,0:T(8,128)(2,1)S(1)}, bf16[4096,512]{1,0:T(8,128)(2,1)}, u32[]{:S(2)}) %copy-start) | copy-done | bytes 4194328
  3.5 0.0 copy-start.1
  3.5 0.8 %copy-done.1 = f32[16,512]{1,0:T(8,128)S(1)} copy-done((f32[16,512]{1,0:T(8,128)S(1)}, f32[16,512]{1,0:T(8,128)}, u32[]{:S(2)}) %copy-start.1) | copy-done | bytes 32792
  4.3 0.0 copy-start.2
  4.3 0.7 %copy-done.2 = s32[4096]{0:T(1024)S(1)} copy-done((s32[4096]{0:T(1024)S(1)}, s32[4096]{0:T(1024)}, u32[]{:S(2)}) %copy-start.2) | copy-done | bytes 16408
  5.0 60.0 %recluster.1 = (f32[16,512]{1,0:T(8,128)S(1)}, f32[2,24]{1,0:T(2,128)S(1)}) custom-call(s32[1,4096]{1,0:T(1,128)S(1)} %bitcast.1, f32[8,128]{1,0:T(8,128)S(1)} %pad.4.refs_1_, f32[16,512]{1,0:T(8,128)S(1)} %copy-done.1, bf16[4096,512]{1,0:T(8,128)(2,1)S(1)} %copy-done), custom_call_target="tpu_custom_call" | custom-call | tf_op jit(solution)/shard_map/recluster/pallas_call | solution.py:528
  65.0 0.6 copy.8
  65.6 0.6 copy.9
  (1 shorter events, 0.0 us)
Async XLA Ops:
  1.3 2.2 %copy-start = (bf16[4096,512]{1,0:T(8,128)(2,1)S(1)}, bf16[4096,512]{1,0:T(8,128)(2,1)}, u32[]{:S(2)}) copy-start(bf16[4096,512]{1,0:T(8,128)(2,1)} %refs_3_.1) | copy-start | bytes 12582916
  3.5 0.8 %copy-start.1 = (f32[16,512]{1,0:T(8,128)S(1)}, f32[16,512]{1,0:T(8,128)}, u32[]{:S(2)}) copy-start(f32[16,512]{1,0:T(8,128)} %refs_2_.1) | copy-start | bytes 98308
  4.3 0.7 %copy-start.2 = (s32[4096]{0:T(1024)S(1)}, s32[4096]{0:T(1024)}, u32[]{:S(2)}) copy-start(s32[4096]{0:T(1024)} %param.5) | copy-start | bytes 49156

commit v2 on v1

--- a/solution.py
+++ b/solution.py
@@ -12,9 +12,6 @@
 OWN = 24
 ROWS = NX * OWN
 BLOCKS = NZ * NC
-HEAD = 40
-TAIL = ROWS - HEAD
-CUT = 64
 LANE = 128
 ORDER = ((4, 3), (-3, 2), (-2, 1), (-1, 0))
 
@@ -45,10 +42,11 @@
 
 def kernel(
     depth, width, features,
-    owner_ref, assign_ref, init_ref, emb_hbm,
+    owner_hbm, assign_hbm, init_hbm, emb_hbm,
     cent_ref, spread_ref,
-    emb, part, other, other_in, xin, zr, zl, qr, ql, hx,
-    prow, info, info_x, group, info_z, counts, match, weight, pad, wrows,
+    owner_ref, assign_ref, init_ref,
+    emb, part, other, other_in, xin, zin,
+    prow, tile, info, info_x, group, info_z, counts, match, weight, pad, wrows,
     table, sq_own, sq_in, scale, scale2, scaled, final_own, final_in, sel, sel_in, lens,
     load_sem, send_sem, recv_sem,
 ):
@@ -105,7 +103,13 @@
         )
         for k in range(chunks)
     ]
-    for load in loads:
+    small = [
+        pltpu.make_async_copy(src, dst, load_sem.at[chunks + k])
+        for k, (src, dst) in enumerate(
+            ((owner_hbm, owner_ref), (assign_hbm, assign_ref), (init_hbm, init_ref))
+        )
+    ]
+    for load in small + loads:
         load.start()
 
     barrier = pltpu.get_barrier_semaphore()
@@ -120,27 +124,31 @@
     greet(0, 12, lambda j: device(dx=lax.div(j, 3), dy=lax.rem(j, 3) + 1))
     greet(2, 16, lambda j: device(dz=lax.div(j, 2), dc=lax.rem(j, 2)))
 
+    tile[...] = jnp.zeros_like(tile)
+    part[...] = jnp.zeros_like(part)
+    other[...] = jnp.zeros_like(other)
+    for load in small:
+        load.wait()
     block, place = position(owner_ref[...])
     prow[...] = block * ROWS + place
-    samples = owner_ref.shape[1]
-    high = lax.broadcasted_iota(jnp.int32, (BLOCKS, samples), 0) == block
-    low = lax.broadcasted_iota(jnp.int32, (LANE, samples), 0) == place
-    info[0:BLOCKS, :] = lax.dot_general(
-        jnp.where(high, 1.0, 0.0).astype(jnp.bfloat16),
-        jnp.where(low, 1.0, 0.0).astype(jnp.bfloat16),
-        (((1,), (1,)), ((), ())), preferred_element_type=jnp.float32,
-    )
-    placed = pltpu.roll(assign_ref[...], x * OWN, 1)
-    info[BLOCKS : BLOCKS + 8, :] = jnp.where(c == 0, placed, pltpu.roll(placed, 2, 0))
-    part[...] = jnp.zeros_like(part)
-    other[...] = jnp.zeros_like(other)
-
-    pl.semaphore_wait(barrier, 7 + 12 + 14)
-
-    arrived = go_all(
-        1, 8, lambda j: (info, info_x.at[j], device(dx=lax.div(j, 2), dc=lax.rem(j, 2)))
-    )
-    info_x[0] = info[...]
+
+    def count():
+        samples = owner_ref.shape[1]
+        block, place = position(owner_ref[...])
+        high = lax.broadcasted_iota(jnp.int32, (BLOCKS, samples), 0) == block
+        low = lax.broadcasted_iota(jnp.int32, (LANE, samples), 0) == place
+        info[0:BLOCKS, :] = lax.dot_general(
+            jnp.where(high, 1.0, 0.0).astype(jnp.bfloat16),
+            jnp.where(low, 1.0, 0.0).astype(jnp.bfloat16),
+            (((1,), (1,)), ((), ())), preferred_element_type=jnp.float32,
+        )
+        tile[0:2, 0:OWN] = assign_ref[...].astype(jnp.float32)
+        placed = pltpu.roll(tile[...], x * OWN, 1)
+        info[BLOCKS : BLOCKS + 8, :] = jnp.where(c == 0, placed, pltpu.roll(placed, 2, 0))
+        info_x[0] = info[...]
+        return go_all(
+            1, 8, lambda j: (info, info_x.at[j], device(dx=lax.div(j, 2), dc=lax.rem(j, 2)))
+        )
 
     def sums(slabs, core, into, waits=()):
         bases = [slab * (NC * ROWS) + core * ROWS for slab in slabs]
@@ -166,96 +174,73 @@
 
     cross = {}
 
-    def work(g):
+    def work_other(g):
         slabs = [zat(d) for d in ORDER[g]]
         sums(slabs, 1 - c, [other.at[g, 0], other.at[g, 1]], loads if g == 0 else ())
+        if g == 0:
+            pl.semaphore_wait(barrier, 7 + 12 + 14)
         cross[g] = go(other.at[g], other_in.at[g], device(dc=1))
-        sums(slabs, c, [part.at[slab] for slab in slabs])
+
+    def work_own(g):
+        sums([zat(d) for d in ORDER[g]], c, [part.at[g, 0], part.at[g, 1]])
 
     def meet(g):
         cross[g].wait_recv()
-        for j, d in enumerate(ORDER[g]):
-            part[zat(d)] += other_in[g, j]
-
-    tail = pl.ds(HEAD, TAIL)
+        part[g] += other_in[g]
+
     xs = {}
 
     def x_start(g):
-        first, second = (zat(d) for d in ORDER[g])
         right, left = device(dx=1), device(dx=-1)
-        xs[g, 0] = go(part.at[first, xat(2), tail], xin.at[g, 0], right)
-        xs[g, 3] = go(part.at[second, xat(2), tail], xin.at[g, 3], left)
-        xs[g, 1] = go(part.at[second, xat(1), tail], xin.at[g, 1], right)
-        xs[g, 4] = go(part.at[first, xat(-1), tail], xin.at[g, 4], left)
+        xs[g, 0] = go(part.at[g, 0, xat(2)], xin.at[g, 0], right)
+        xs[g, 3] = go(part.at[g, 1, xat(2)], xin.at[g, 3], left)
+        xs[g, 1] = go(part.at[g, 1, xat(1)], xin.at[g, 1], right)
+        xs[g, 4] = go(part.at[g, 0, xat(-1)], xin.at[g, 4], left)
 
     def x_mid(g):
-        first, second = (zat(d) for d in ORDER[g])
         xs[g, 0].wait_recv()
-        part[first, xat(1), HEAD:ROWS] += xin[g, 0]
-        xs[g, 2] = go(part.at[first, xat(1), tail], xin.at[g, 2], device(dx=1))
+        part[g, 0, xat(1)] += xin[g, 0]
+        xs[g, 2] = go(part.at[g, 0, xat(1)], xin.at[g, 2], device(dx=1))
         xs[g, 3].wait_recv()
-        part[second, xat(-1), HEAD:ROWS] += xin[g, 3]
-        xs[g, 5] = go(part.at[second, xat(-1), tail], xin.at[g, 5], device(dx=-1))
+        part[g, 1, xat(-1)] += xin[g, 3]
+        xs[g, 5] = go(part.at[g, 1, xat(-1)], xin.at[g, 5], device(dx=-1))
+
+    def x_direct(g):
+        for k, d in enumerate((2, 1, -1)):
+            at = pl.ds(2 * k, 2)
+            xs[g, k] = go(part.at[g, :, xat(d)], xin.at[g, at], device(dx=d))
+
+    zs = {}
+
+    def z_send(g, j):
+        d = ORDER[g][j]
+        if d != 0:
+            zs[g, j] = go(part.at[g, j, x], zin.at[2 * g + j], device(dz=d))
 
     def x_end(g):
-        first, second = (zat(d) for d in ORDER[g])
         xs[g, 4].wait_recv()
         xs[g, 2].wait_recv()
-        part[first, x, HEAD:ROWS] += xin[g, 4] + xin[g, 2]
+        part[g, 0, x] += xin[g, 4] + xin[g, 2]
+        z_send(g, 0)
         xs[g, 1].wait_recv()
         xs[g, 5].wait_recv()
-        part[second, x, HEAD:ROWS] += xin[g, 1] + xin[g, 5]
-
-    head = pl.ds(0, HEAD)
-    zs = {}
-
-    def z_head(h, way):
-        slab = zat((4 - h) * way)
-        into, half = (zr, 0) if way > 0 else (zl, 2)
-        if h == 0:
-            at = pl.ds(half, 2)
-            zs[h, way] = go(part.at[slab, at, head], into.at[0, at], device(dz=way))
-            return
-        zs[h - 1, way].wait_recv()
-        if h == 1:
-            part[slab, half : half + 2, 0:HEAD] += into[0, half : half + 2]
-        else:
-            part[slab, :, 0:HEAD] += into[h - 1]
-        zs[h, way] = go(part.at[slab, :, head], into.at[h], device(dz=way))
-
-    def z_head_end():
-        zs[3, 1].wait_recv()
-        zs[3, -1].wait_recv()
-        part[z, :, 0:HEAD] += zr[3] + zl[3]
-
-    ts = {}
-
-    def z_tail(h, way):
-        slab = zat((4 - h) * way)
-        into, start, size = (qr, HEAD, CUT - HEAD) if way > 0 else (ql, CUT, ROWS - CUT)
-        if h == 0:
-            ts[h, way] = go(
-                part.at[slab, x, pl.ds(start, size)], into.at[0, pl.ds(0, size)], device(dz=way)
-            )
-            return
-        ts[h - 1, way].wait_recv()
-        if h == 1:
-            part[slab, x, start : start + size] += into[0, 0:size]
-        else:
-            part[slab, x, HEAD:ROWS] += into[h - 1]
-        ts[h, way] = go(part.at[slab, x, tail], into.at[h], device(dz=way))
-
-    def z_tail_end():
-        ts[3, 1].wait_recv()
-        ts[3, -1].wait_recv()
-        part[z, x, HEAD:ROWS] += qr[3] + ql[3]
-
-    work(0)
+        part[g, 1, x] += xin[g, 1] + xin[g, 5]
+        z_send(g, 1)
+
+    def x_direct_end(g):
+        for k in range(3):
+            xs[g, k].wait_recv()
+        for j in range(2):
+            part[g, j, x] += xin[g, j] + xin[g, 2 + j] + xin[g, 4 + j]
+            z_send(g, j)
+
+    work_other(0)
+    arrived = count()
+    work_own(0)
     meet(0)
-    z_head(0, 1)
-    z_head(0, -1)
     x_start(0)
 
+    work_other(1)
     arrived()
     whole = info_x[0]
     for j in range(1, NX * NC):
@@ -263,76 +248,46 @@
     group[...] = whole
     info_z[z] = whole
     arrived_z = go_all(1, NZ, lambda j: (group, info_z.at[z], device(dz=j)))
-
-    work(1)
+    work_own(1)
     meet(1)
-    z_head(1, 1)
-    z_head(1, -1)
+    x_start(1)
+
+    work_other(2)
     x_mid(0)
-    x_start(1)
-
-    work(2)
+    work_own(2)
     meet(2)
-    z_head(2, 1)
-    z_head(2, -1)
+    x_start(2)
+
+    work_other(3)
     x_mid(1)
-    x_start(2)
     x_end(0)
-    z_tail(0, 1)
-    z_tail(0, -1)
-
-    work(3)
+    work_own(3)
     meet(3)
-    z_head(3, 1)
-    z_head(3, -1)
+    x_direct(3)
     x_mid(2)
-    x_start(3)
     x_end(1)
-    z_tail(1, 1)
-    z_tail(1, -1)
-    x_mid(3)
     x_end(2)
-    z_tail(2, 1)
-    z_tail(2, -1)
-    z_head_end()
-    hop = go(part.at[z, xat(2), head], hx.at[0], device(dx=1))
-    back = go(part.at[z, xat(-1), head], hx.at[1], device(dx=-1))
-    x_end(3)
-    z_tail(3, 1)
-    z_tail(3, -1)
-    hop.wait_recv()
-    part[z, xat(1), 0:HEAD] += hx[0]
-    last = go(part.at[z, xat(1), head], hx.at[2], device(dx=1))
-    z_tail_end()
-    back.wait_recv()
-    last.wait_recv()
-    part[z, x, 0:HEAD] += hx[1] + hx[2]
-
-    own = part[z, x]
+    x_direct_end(3)
+    own = part[3, 1, x]
+    for g in range(4):
+        for j in range(2):
+            if (g, j) in zs:
+                zs[g, j].wait_recv()
+                own = own + zin[2 * g + j]
+
     mine = z * NC + c
     table[mine] = own
-
-    rings = {}
+    rings, pairs = {}, []
 
     def blk(dz):
         return zat(dz) * NC + c
-
-    def z_share(h, way):
-        at = blk(-h * way)
-        if h == 3:
-            rows = pl.ds(0, ROWS // 2) if way > 0 else pl.ds(ROWS // 2, ROWS // 2)
-        else:
-            rows = pl.ds(0, ROWS)
-        rings[h, way] = go(table.at[at, rows], table.at[at, rows], device(dz=way))
-
-    pairs = []
 
     def core_share(dz):
         at = blk(dz)
         pairs.append(go(table.at[at], table.at[at], device(dc=1)))
 
-    z_share(0, 1)
-    z_share(0, -1)
+    for dz in (4, 3, -3, 2, -2, 1, -1):
+        rings[dz] = go(table.at[mine], table.at[mine], device(dz=dz))
     core_share(0)
 
     square = jnp.sum(own * own, axis=1, keepdims=True)
@@ -347,12 +302,6 @@
     for j in range(1, NZ):
         total = total + info_z[j, 0:BLOCKS]
     counts[...] = total
-
-    for way in (1, -1):
-        rings[0, way].wait_recv()
-        z_share(1, way)
-    core_share(-1)
-    core_share(1)
 
     keys_all = group[BLOCKS : BLOCKS + 8, :]
     keys = as_columns(jnp.where(c == 0, keys_all, pltpu.roll(keys_all, 6, 0)))
@@ -393,24 +342,14 @@
     )
     means = own * as_columns(jnp.broadcast_to(inverse, (8, LANE)))[0:ROWS, 0:1]
 
-    for way in (1, -1):
-        rings[1, way].wait_recv()
-        z_share(2, way)
-    core_share(-2)
-    core_share(2)
-    for way in (1, -1):
-        rings[2, way].wait_recv()
-        z_share(3, way)
-    core_share(-3)
-    core_share(3)
+    for dz in (-1, 1, -2, 2, -3, 3, 4):
+        rings[dz].wait_recv()
+        core_share(-dz)
 
     scale_arrived()
     for b in range(BLOCKS):
         scale2[b : b + 1, :] = scale[b]
     factor = as_columns(counts[...] * scale2[...])
-    rings[3, 1].wait_recv()
-    rings[3, -1].wait_recv()
-    core_share(4)
     for pair in pairs:
         pair.wait_recv()
     scaled[...] = jnp.zeros_like(scaled)
@@ -472,29 +411,29 @@
         wait()
 
 
-COPIES = 7 + 7 + 4 + 24 + 8 + 8 + 3 + 8 + 8 + 15 + 15 + 15 + 3
+COPIES = 7 + 7 + 4 + 21 + 7 + 7 + 8 + 15 + 15 + 15 + 3
 
 
 def per_device(features, embeddings, sample_owner, lloyd_assign, init_centroids):
     samples, width = embeddings.shape
     per = init_centroids.shape[0]
-    depth = 1024
+    depth = 2048
     f32, bf16 = jnp.float32, jnp.bfloat16
     vm = pltpu.VMEM
     cents = NX * per
     lines = 2 * (cents + ROWS)
     scratch = [
+        vm((1, samples), jnp.int32),
+        vm((2, OWN), jnp.int32),
+        vm((per, width), f32),
         vm((samples, width), bf16),
-        vm((NZ, NX, ROWS, LANE), f32),
         vm((4, 2, NX, ROWS, LANE), f32),
         vm((4, 2, NX, ROWS, LANE), f32),
-        vm((4, 6, TAIL, LANE), f32),
-        vm((4, NX, HEAD, LANE), f32),
-        vm((4, NX, HEAD, LANE), f32),
-        vm((4, TAIL, LANE), f32),
-        vm((4, TAIL, LANE), f32),
-        vm((3, HEAD, LANE), f32),
+        vm((4, 2, NX, ROWS, LANE), f32),
+        vm((4, 6, ROWS, LANE), f32),
+        vm((NZ, ROWS, LANE), f32),
         vm((1, samples), jnp.int32),
+        vm((8, LANE), f32),
         vm((24, LANE), f32),
         vm((NX * NC, 24, LANE), f32),
         vm((24, LANE), f32),
@@ -515,11 +454,10 @@
         vm((cents, LANE), f32),
         vm((NX, per, LANE), f32),
         vm((LANE, 8), f32),
-        pltpu.SemaphoreType.DMA((samples // depth,)),
+        pltpu.SemaphoreType.DMA((samples // depth + 3,)),
         pltpu.SemaphoreType.DMA((COPIES,)),
         pltpu.SemaphoreType.DMA((COPIES,)),
     ]
-    assign = jnp.pad(lloyd_assign.astype(f32), ((0, 6), (0, LANE - OWN)))
     in_vmem = pl.BlockSpec(memory_space=pltpu.VMEM)
 
     def body(*refs):
@@ -532,13 +470,13 @@
             jax.ShapeDtypeStruct((per, width), f32),
             jax.ShapeDtypeStruct((2, OWN), f32),
         ),
-        in_specs=[in_vmem, in_vmem, in_vmem, pl.BlockSpec(memory_space=pltpu.HBM)],
+        in_specs=[pl.BlockSpec(memory_space=pl.ANY)] * 4,
         out_specs=(in_vmem, in_vmem),
         scratch_shapes=scratch,
         compiler_params=pltpu.CompilerParams(
-            collective_id=0, has_side_effects=True, vmem_limit_bytes=48 << 20
+            collective_id=0, has_side_effects=True, vmem_limit_bytes=60 << 20
         ),
-    )(sample_owner.reshape(1, samples), assign, init_centroids, embeddings)
+    )(sample_owner.reshape(1, samples), lloyd_assign, init_centroids, embeddings)
 
 
 def solution(mesh):

time: 66.4 us -> 58.4 us (0.88)
  Pallas kernels: 60 us -> 55 us
  local copies, waits for them, and re-layouts: 4.85 us -> 2.6 us
  other arithmetic: 0.68 us -> 0 us
    pallas_call x1, Pallas kernels: 60 us -> 55 us  [per_device(): pl.pallas_call(body, name='recluster', out_shape=(jax.ShapeDtypeStruct((p...]
    unnamed x8 -> x2, local copies, waits for them, and re-layouts: 4.84 us -> 2.6 us
    convert_element_type x1 -> x0, other arithmetic: 0.68 us -> none  [per_device(): assign = jnp.pad(lloyd_assign.astype(f32), ((0, 6), (0, LANE - OWN)))]
where the time goes in v2:
time: 58.4 us; the launch traced here: 58.3 us
  Pallas kernels  55 us (94%)
  local copies, waits for them, and re-layouts  2.6 us (4%)
  between operations  0.64 us (1%)
    pallas_call x1, Pallas kernels, per_device(): pl.pallas_call(body, name='recluster', out_shape=(jax.ShapeDtypeStruct((p...  55 us
    unnamed x2, local copies, waits for them, and re-layouts  2.6 us

profile of v2, /device:TPU:1, one launch (start us, length us, event | category | flops | bytes accessed | tf_op | source)
XLA Modules:
  0.0 58.3 jit_solution(13017560417911438186)
XLA Ops:
  0.6 55.0 %recluster.1 = (f32[16,512]{1,0:T(8,128)}, f32[2,24]{1,0:T(2,128)}) custom-call(s32[1,4096]{1,0:T(1,128)} %bitcast.1, s32[2,24]{1,0:T(2,128)} %refs_1_.1, f32[16,512]{1,0:T(8,128)} %refs_2_.1, bf16[4096,512]{1,0:T(8,128)(2,1)} %refs_3_.1), custom_call_target="tpu_custom_call" | custom-call | tf_op jit(solution)/shard_map/recluster/pallas_call | solution.py:466
  55.7 1.4 %copy.8 = f32[16,512]{1,0:T(8,128)} copy(f32[16,512]{1,0:T(8,128)} %get-tuple-element.4) | data formatting | bytes 65536
  57.0 1.2 %copy.9 = f32[2,24]{1,0:T(2,128)} copy(f32[2,24]{1,0:T(2,128)} %get-tuple-element.5) | data formatting | bytes 384

commit v3 on v2

--- a/solution.py
+++ b/solution.py
@@ -13,7 +13,7 @@
 ROWS = NX * OWN
 BLOCKS = NZ * NC
 LANE = 128
-ORDER = ((4, 3), (-3, 2), (-2, 1), (-1, 0))
+ORDER = (4, 3, -3, 2, -2, 1, -1, 0)
 
 
 def position(owner):
@@ -150,8 +150,7 @@
             1, 8, lambda j: (info, info_x.at[j], device(dx=lax.div(j, 2), dc=lax.rem(j, 2)))
         )
 
-    def sums(slabs, core, into, waits=()):
-        bases = [slab * (NC * ROWS) + core * ROWS for slab in slabs]
+    def sums(bases, into, waits=()):
         row = lax.broadcasted_iota(jnp.int32, (ROWS, depth), 0)
 
         def step(k):
@@ -174,73 +173,75 @@
 
     cross = {}
 
-    def work_other(g):
-        slabs = [zat(d) for d in ORDER[g]]
-        sums(slabs, 1 - c, [other.at[g, 0], other.at[g, 1]], loads if g == 0 else ())
-        if g == 0:
-            pl.semaphore_wait(barrier, 7 + 12 + 14)
-        cross[g] = go(other.at[g], other_in.at[g], device(dc=1))
-
-    def work_own(g):
-        sums([zat(d) for d in ORDER[g]], c, [part.at[g, 0], part.at[g, 1]])
-
-    def meet(g):
-        cross[g].wait_recv()
-        part[g] += other_in[g]
+    def work(s):
+        base = zat(ORDER[s]) * (NC * ROWS)
+        bases = [base + (1 - c) * ROWS, base + c * ROWS]
+        sums(bases, [other.at[s], part.at[s]], loads if s == 0 else ())
+
+    def give(s):
+        cross[s] = go(other.at[s], other_in.at[s], device(dc=1))
+
+    def meet(s):
+        cross[s].wait_recv()
+        part[s] += other_in[s]
 
     xs = {}
 
-    def x_start(g):
-        right, left = device(dx=1), device(dx=-1)
-        xs[g, 0] = go(part.at[g, 0, xat(2)], xin.at[g, 0], right)
-        xs[g, 3] = go(part.at[g, 1, xat(2)], xin.at[g, 3], left)
-        xs[g, 1] = go(part.at[g, 1, xat(1)], xin.at[g, 1], right)
-        xs[g, 4] = go(part.at[g, 0, xat(-1)], xin.at[g, 4], left)
-
-    def x_mid(g):
-        xs[g, 0].wait_recv()
-        part[g, 0, xat(1)] += xin[g, 0]
-        xs[g, 2] = go(part.at[g, 0, xat(1)], xin.at[g, 2], device(dx=1))
-        xs[g, 3].wait_recv()
-        part[g, 1, xat(-1)] += xin[g, 3]
-        xs[g, 5] = go(part.at[g, 1, xat(-1)], xin.at[g, 5], device(dx=-1))
-
-    def x_direct(g):
+    def x_start(s):
+        xs[s, 0] = go(part.at[s, xat(2)], xin.at[s, 0], device(dx=-1))
+        xs[s, 1] = go(part.at[s, xat(1)], xin.at[s, 1], device(dx=1))
+
+    def x_mid(s):
+        xs[s, 0].wait_recv()
+        part[s, xat(-1)] += xin[s, 0]
+        xs[s, 2] = go(part.at[s, xat(-1)], xin.at[s, 2], device(dx=-1))
+
+    def x_direct(s):
         for k, d in enumerate((2, 1, -1)):
-            at = pl.ds(2 * k, 2)
-            xs[g, k] = go(part.at[g, :, xat(d)], xin.at[g, at], device(dx=d))
+            xs[s, k] = go(part.at[s, xat(d)], xin.at[s, k], device(dx=d))
 
     zs = {}
-
-    def z_send(g, j):
-        d = ORDER[g][j]
+    hops = {4: 2, 3: 1, -3: -1}
+
+    def x_end(s):
+        d = ORDER[s]
+        if (s, 0) in direct:
+            xs[s, 0].wait_recv()
+        xs[s, 1].wait_recv()
+        xs[s, 2].wait_recv()
+        total = part[s, x] + xin[s, 1] + xin[s, 2]
+        if (s, 0) in direct:
+            total = total + xin[s, 0]
+        for far in {2: (4, 3), -2: (-3,)}.get(d, ()):
+            zs[far].wait_recv()
+            total = total + zin[ORDER.index(far)]
+        part[s, x] = total
         if d != 0:
-            zs[g, j] = go(part.at[g, j, x], zin.at[2 * g + j], device(dz=d))
-
-    def x_end(g):
-        xs[g, 4].wait_recv()
-        xs[g, 2].wait_recv()
-        part[g, 0, x] += xin[g, 4] + xin[g, 2]
-        z_send(g, 0)
-        xs[g, 1].wait_recv()
-        xs[g, 5].wait_recv()
-        part[g, 1, x] += xin[g, 1] + xin[g, 5]
-        z_send(g, 1)
-
-    def x_direct_end(g):
-        for k in range(3):
-            xs[g, k].wait_recv()
-        for j in range(2):
-            part[g, j, x] += xin[g, j] + xin[g, 2 + j] + xin[g, 4 + j]
-            z_send(g, j)
-
-    work_other(0)
+            zs[d] = go(part.at[s, x], zin.at[s], device(dz=hops.get(d, d)))
+
+    direct = {(s, 0) for s in (0, 1, 6, 7)}
+
+    work(0)
+    work(1)
+    pl.semaphore_wait(barrier, 7 + 12 + 14)
+    give(0)
+    give(1)
     arrived = count()
-    work_own(0)
+
+    work(2)
+    give(2)
     meet(0)
-    x_start(0)
-
-    work_other(1)
+    x_direct(0)
+    meet(1)
+    x_direct(1)
+    work(3)
+    give(3)
+    meet(2)
+    x_start(2)
+    work(4)
+    give(4)
+    meet(3)
+    x_start(3)
     arrived()
     whole = info_x[0]
     for j in range(1, NX * NC):
@@ -248,32 +249,36 @@
     group[...] = whole
     info_z[z] = whole
     arrived_z = go_all(1, NZ, lambda j: (group, info_z.at[z], device(dz=j)))
-    work_own(1)
-    meet(1)
-    x_start(1)
-
-    work_other(2)
-    x_mid(0)
-    work_own(2)
-    meet(2)
-    x_start(2)
-
-    work_other(3)
-    x_mid(1)
+    work(5)
+    give(5)
+    meet(4)
+    x_start(4)
+    x_mid(2)
     x_end(0)
-    work_own(3)
-    meet(3)
-    x_direct(3)
-    x_mid(2)
+    work(6)
+    give(6)
+    meet(5)
+    x_start(5)
     x_end(1)
+    x_mid(3)
+    work(7)
+    give(7)
+    meet(6)
+    x_direct(6)
+    x_mid(4)
     x_end(2)
-    x_direct_end(3)
-    own = part[3, 1, x]
-    for g in range(4):
-        for j in range(2):
-            if (g, j) in zs:
-                zs[g, j].wait_recv()
-                own = own + zin[2 * g + j]
+    meet(7)
+    x_direct(7)
+    x_mid(5)
+    x_end(3)
+    x_end(4)
+    x_end(6)
+    x_end(5)
+    x_end(7)
+    own = part[7, x]
+    for d in (2, -2, -1, 1):
+        zs[d].wait_recv()
+        own = own + zin[ORDER.index(d)]
 
     mine = z * NC + c
     table[mine] = own
@@ -411,7 +416,7 @@
         wait()
 
 
-COPIES = 7 + 7 + 4 + 21 + 7 + 7 + 8 + 15 + 15 + 15 + 3
+COPIES = 7 + 7 + 8 + 24 + 7 + 7 + 8 + 15 + 15 + 15 + 3
 
 
 def per_device(features, embeddings, sample_owner, lloyd_assign, init_centroids):
@@ -427,10 +432,10 @@
         vm((2, OWN), jnp.int32),
         vm((per, width), f32),
         vm((samples, width), bf16),
-        vm((4, 2, NX, ROWS, LANE), f32),
-        vm((4, 2, NX, ROWS, LANE), f32),
-        vm((4, 2, NX, ROWS, LANE), f32),
-        vm((4, 6, ROWS, LANE), f32),
+        vm((NZ, NX, ROWS, LANE), f32),
+        vm((NZ, NX, ROWS, LANE), f32),
+        vm((NZ, NX, ROWS, LANE), f32),
+        vm((NZ, 3, ROWS, LANE), f32),
         vm((NZ, ROWS, LANE), f32),
         vm((1, samples), jnp.int32),
         vm((8, LANE), f32),

time: 58.4 us -> 59.2 us (1.014)
  Pallas kernels: 55 us -> 55.8 us
    pallas_call x1, Pallas kernels: 55 us -> 55.8 us  [per_device(): pl.pallas_call(body, name='recluster', out_shape=(jax.ShapeDtypeStruct((p...]
where the time goes in v3:
time: 59.2 us; the launch traced here: 59 us
  Pallas kernels  55.8 us (94%)
  local copies, waits for them, and re-layouts  2.6 us (4%)
  between operations  0.64 us (1%)
    pallas_call x1, Pallas kernels, per_device(): pl.pallas_call(body, name='recluster', out_shape=(jax.ShapeDtypeStruct((p...  55.8 us
    unnamed x2, local copies, waits for them, and re-layouts  2.6 us

profile of v3, /device:TPU:1, one launch (start us, length us, event | category | flops | bytes accessed | tf_op | source)
XLA Modules:
  0.0 59.0 jit_solution(14981232222754275622)
XLA Ops:
  0.6 55.8 %recluster.1 = (f32[16,512]{1,0:T(8,128)}, f32[2,24]{1,0:T(2,128)}) custom-call(s32[1,4096]{1,0:T(1,128)} %bitcast.1, s32[2,24]{1,0:T(2,128)} %refs_1_.1, f32[16,512]{1,0:T(8,128)} %refs_2_.1, bf16[4096,512]{1,0:T(8,128)(2,1)} %refs_3_.1), custom_call_target="tpu_custom_call" | custom-call | tf_op jit(solution)/shard_map/recluster/pallas_call | solution.py:471
  56.4 1.4 %copy.8 = f32[16,512]{1,0:T(8,128)} copy(f32[16,512]{1,0:T(8,128)} %get-tuple-element.4) | data formatting | bytes 65536
  57.8 1.2 %copy.9 = f32[2,24]{1,0:T(2,128)} copy(f32[2,24]{1,0:T(2,128)} %get-tuple-element.5) | data formatting | bytes 384

commit v4 on v3

--- a/solution.py
+++ b/solution.py
@@ -13,7 +13,7 @@
 ROWS = NX * OWN
 BLOCKS = NZ * NC
 LANE = 128
-ORDER = (4, 3, -3, 2, -2, 1, -1, 0)
+ORDER = (4, 3, -3, 1, -1, 2, -2, 0)
 
 
 def position(owner):
@@ -45,7 +45,7 @@
     owner_hbm, assign_hbm, init_hbm, emb_hbm,
     cent_ref, spread_ref,
     owner_ref, assign_ref, init_ref,
-    emb, part, other, other_in, xin, zin,
+    emb, part, other, other_in, xin, zslab, zin,
     prow, tile, info, info_x, group, info_z, counts, match, weight, pad, wrows,
     table, sq_own, sq_in, scale, scale2, scaled, final_own, final_in, sel, sel_in, lens,
     load_sem, send_sem, recv_sem,
@@ -219,7 +219,7 @@
         if d != 0:
             zs[d] = go(part.at[s, x], zin.at[s], device(dz=hops.get(d, d)))
 
-    direct = {(s, 0) for s in (0, 1, 6, 7)}
+    direct = {(s, 0) for s in (6, 7)}
 
     work(0)
     work(1)
@@ -228,12 +228,18 @@
     give(1)
     arrived = count()
 
+    whole_slab = {}
+
+    def z_whole(s):
+        d = ORDER[s]
+        whole_slab[s] = go(part.at[s], zslab.at[s - 3], device(dz=d))
+
     work(2)
     give(2)
     meet(0)
-    x_direct(0)
+    x_start(0)
     meet(1)
-    x_direct(1)
+    x_start(1)
     work(3)
     give(3)
     meet(2)
@@ -241,7 +247,7 @@
     work(4)
     give(4)
     meet(3)
-    x_start(3)
+    z_whole(3)
     arrived()
     whole = info_x[0]
     for j in range(1, NX * NC):
@@ -252,31 +258,32 @@
     work(5)
     give(5)
     meet(4)
-    x_start(4)
-    x_mid(2)
-    x_end(0)
+    z_whole(4)
+    x_mid(0)
+    x_mid(1)
     work(6)
     give(6)
     meet(5)
     x_start(5)
-    x_end(1)
-    x_mid(3)
+    x_mid(2)
     work(7)
     give(7)
     meet(6)
     x_direct(6)
-    x_mid(4)
-    x_end(2)
-    meet(7)
+    x_end(0)
+    x_end(1)
+    cross[7].wait_recv()
+    whole_slab[3].wait_recv()
+    whole_slab[4].wait_recv()
+    part[7] += other_in[7] + zslab[0] + zslab[1]
     x_direct(7)
     x_mid(5)
-    x_end(3)
-    x_end(4)
+    x_end(2)
     x_end(6)
     x_end(5)
     x_end(7)
     own = part[7, x]
-    for d in (2, -2, -1, 1):
+    for d in (2, -2):
         zs[d].wait_recv()
         own = own + zin[ORDER.index(d)]
 
@@ -291,7 +298,7 @@
         at = blk(dz)
         pairs.append(go(table.at[at], table.at[at], device(dc=1)))
 
-    for dz in (4, 3, -3, 2, -2, 1, -1):
+    for dz in (2, -2, 1, -1):
         rings[dz] = go(table.at[mine], table.at[mine], device(dz=dz))
     core_share(0)
 
@@ -307,6 +314,18 @@
     for j in range(1, NZ):
         total = total + info_z[j, 0:BLOCKS]
     counts[...] = total
+
+    half = ROWS // 2
+    for way in (1, -1):
+        rings[2 * way].wait_recv()
+        at = blk(-2 * way)
+        rings[3 * way] = go(table.at[at], table.at[at], device(dz=way))
+        rows = pl.ds(0 if way > 0 else half, half)
+        rings[4 * way] = go(table.at[at, rows], table.at[at, rows], device(dz=2 * way))
+        core_share(-2 * way)
+    for way in (1, -1):
+        rings[way].wait_recv()
+        core_share(-way)
 
     keys_all = group[BLOCKS : BLOCKS + 8, :]
     keys = as_columns(jnp.where(c == 0, keys_all, pltpu.roll(keys_all, 6, 0)))
@@ -347,9 +366,12 @@
     )
     means = own * as_columns(jnp.broadcast_to(inverse, (8, LANE)))[0:ROWS, 0:1]
 
-    for dz in (-1, 1, -2, 2, -3, 3, 4):
-        rings[dz].wait_recv()
-        core_share(-dz)
+    for way in (1, -1):
+        rings[3 * way].wait_recv()
+        core_share(-3 * way)
+    rings[4].wait_recv()
+    rings[-4].wait_recv()
+    core_share(4)
 
     scale_arrived()
     for b in range(BLOCKS):
@@ -416,7 +438,7 @@
         wait()
 
 
-COPIES = 7 + 7 + 8 + 24 + 7 + 7 + 8 + 15 + 15 + 15 + 3
+COPIES = 7 + 7 + 8 + 18 + 2 + 5 + 8 + 8 + 15 + 15 + 15 + 3
 
 
 def per_device(features, embeddings, sample_owner, lloyd_assign, init_centroids):
@@ -436,6 +458,7 @@
         vm((NZ, NX, ROWS, LANE), f32),
         vm((NZ, NX, ROWS, LANE), f32),
         vm((NZ, 3, ROWS, LANE), f32),
+        vm((2, NX, ROWS, LANE), f32),
         vm((NZ, ROWS, LANE), f32),
         vm((1, samples), jnp.int32),
         vm((8, LANE), f32),
@@ -468,7 +491,7 @@
     def body(*refs):
         kernel(depth, width, features, *refs)
 
-    return pl.pallas_call(
+    packed = pl.pallas_call(
         body,
         name="recluster",
         out_shape=(
@@ -483,6 +506,29 @@
         ),
     )(sample_owner.reshape(1, samples), lloyd_assign, init_centroids, embeddings)
 
+    def hand_out(cent_in, spread_in, cent_out, spread_out, sem):
+        copies = [
+            pltpu.make_async_copy(cent_in, cent_out, sem.at[0]),
+            pltpu.make_async_copy(spread_in, spread_out, sem.at[1]),
+        ]
+        for copy in copies:
+            copy.start()
+        for copy in copies:
+            copy.wait()
+
+    anywhere = pl.BlockSpec(memory_space=pl.ANY)
+    return pl.pallas_call(
+        hand_out,
+        name="hand_out",
+        out_shape=(
+            jax.ShapeDtypeStruct((per, width), f32),
+            jax.ShapeDtypeStruct((2, OWN), f32),
+        ),
+        in_specs=[anywhere] * 2,
+        out_specs=(anywhere, anywhere),
+        scratch_shapes=[pltpu.SemaphoreType.DMA((2,))],
+    )(*packed)
+
 
 def solution(mesh):
     def run(embeddings, sample_owner, lloyd_assign, init_centroids):

time: 59.2 us -> 56.4 us (0.953)
  local copies, waits for them, and re-layouts: 2.6 us -> 0 us
    unnamed x2 -> x0, local copies, waits for them, and re-layouts: 2.6 us -> none
    pallas_call x1, Pallas kernels: 55.8 us -> 53.6 us  [per_device(): pl.pallas_call(body, name='recluster', out_shape=(jax.ShapeDtypeStruct((p...]
    pallas_call x0 -> x1, Pallas kernels: none -> 2.14 us  [per_device(): pl.pallas_call(hand_out, name='hand_out', out_shape=(jax.ShapeDtypeStruct...]
where the time goes in v4:
time: 56.4 us
  Pallas kernels  55.7 us (99%)
  between operations  0.64 us (1%)
    pallas_call x1, Pallas kernels, per_device(): pl.pallas_call(body, name='recluster', out_shape=(jax.ShapeDtypeStruct((p...  53.6 us
    pallas_call x1, Pallas kernels, per_device(): pl.pallas_call(hand_out, name='hand_out', out_shape=(jax.ShapeDtypeStruct...  2.14 us

profile of v4, /device:TPU:1, one launch (start us, length us, event | category | flops | bytes accessed | tf_op | source)
XLA Modules:
  0.0 56.4 jit_solution(9180433844226412154)
XLA Ops:
  0.6 53.6 %recluster.1 = (f32[16,512]{1,0:T(8,128)}, f32[2,24]{1,0:T(2,128)}) custom-call(s32[1,4096]{1,0:T(1,128)} %bitcast.1, s32[2,24]{1,0:T(2,128)} %refs_1_.1, f32[16,512]{1,0:T(8,128)} %refs_2_.1, bf16[4096,512]{1,0:T(8,128)(2,1)} %refs_3_.1), custom_call_target="tpu_custom_call" | custom-call | tf_op jit(solution)/shard_map/recluster/pallas_call | solution.py:494
  54.2 2.1 %hand_out.1 = (f32[16,512]{1,0:T(8,128)}, f32[2,24]{1,0:T(2,128)}) custom-call(f32[16,512]{1,0:T(8,128)} %get-tuple-element.4.cent_in, f32[2,24]{1,0:T(2,128)} %get-tuple-element.5.spread_in), custom_call_target="tpu_custom_call" | custom-call | tf_op jit(solution)/shard_map/hand_out/pallas_call | solution.py:520

commit v5 on v4

--- a/solution.py
+++ b/solution.py
@@ -51,50 +51,59 @@
     load_sem, send_sem, recv_sem,
 ):
     dp, y = lax.axis_index("dp"), lax.axis_index("feat")
-    z, x, c = lax.div(dp, NX * NC), lax.rem(lax.div(dp, NC), NX), lax.rem(dp, NC)
+    z = lax.div(dp, NX * NC)
+    x = lax.div(dp - z * (NX * NC), NC)
+    c = dp - z * (NX * NC) - x * NC
+
+    def around(at, size):
+        steps = [at]
+        for d in range(1, size):
+            steps.append(jnp.where(at + d >= size, at + (d - size), at + d))
+        return steps
+
+    z_at, x_at, c_at, y_at = around(z, NZ), around(x, NX), around(c, NC), around(y, NY)
+    z_first = [at * (NX * NC) for at in z_at]
+    x_first = [at * NC for at in x_at]
 
     def zat(d):
-        return lax.rem(z + d + NZ, NZ)
+        return z_at[d % NZ]
 
     def xat(d):
-        return lax.rem(x + d + NX, NX)
+        return x_at[d % NX]
 
     def device(dz=0, dx=0, dc=0, dy=0):
-        return (zat(dz) * (NX * NC) + xat(dx) * NC + lax.rem(c + dc, NC), lax.rem(y + dy, NY))
+        return (z_first[dz % NZ] + (x_first[dx % NX] + c_at[dc % NC]), y_at[dy % NY])
 
     used = [0]
     sent = []
 
-    def copy_at(slot, src, dst, to):
-        return pltpu.make_async_remote_copy(
+    def go(src, dst, to):
+        slot = used[0]
+        used[0] += 1
+        copy = pltpu.make_async_remote_copy(
             src_ref=src, dst_ref=dst, send_sem=send_sem.at[slot], recv_sem=recv_sem.at[slot],
             device_id=to, device_id_type=MESH,
         )
-
-    def go(src, dst, to):
-        copy = copy_at(used[0], src, dst, to)
-        used[0] += 1
         copy.start()
         sent.append(copy.wait_send)
         return copy
 
-    def go_all(first, last, make):
-        base = used[0]
-        used[0] += last - first
-
-        def at(j):
-            src, dst, to = make(j)
-            return copy_at(base + j - first, src, dst, to)
-
-        def run(act):
-            def step(j, carry):
-                act(at(j))
-                return carry
-            lax.fori_loop(first, last, step, 0)
-
-        run(lambda copy: copy.start())
-        sent.append(lambda: run(lambda copy: copy.wait_send()))
-        return lambda: run(lambda copy: copy.wait_recv())
+    def go_all(makes):
+        copies = [go(*make) for make in makes]
+
+        def wait():
+            for copy in copies:
+                copy.wait_recv()
+
+        return wait
+
+    group_xc = [(dx, dc) for dx in (2, 1, 3, 0) for dc in range(NC) if (dx, dc) != (0, 0)]
+    group_xy = [
+        (dx, dy) for dx in (2, 1, 3, 0) for dy in (2, 1, 3, 0) if (dx, dy) != (0, 0)
+    ]
+    group_zc = [
+        (dz, dc) for dz in (4, 3, 5, 2, 6, 1, 7, 0) for dc in range(NC) if (dz, dc) != (0, 0)
+    ]
 
     chunks = emb.shape[0] // depth
     loads = [
@@ -114,15 +123,10 @@
 
     barrier = pltpu.get_barrier_semaphore()
 
-    def greet(first, last, to):
-        def step(j, carry):
-            pl.semaphore_signal(barrier, inc=1, device_id=to(j), device_id_type=MESH)
-            return carry
-        lax.fori_loop(first, last, step, 0)
-
-    greet(1, 8, lambda j: device(dx=lax.div(j, 2), dc=lax.rem(j, 2)))
-    greet(0, 12, lambda j: device(dx=lax.div(j, 3), dy=lax.rem(j, 3) + 1))
-    greet(2, 16, lambda j: device(dz=lax.div(j, 2), dc=lax.rem(j, 2)))
+    greeted = {(dz, 0, dc, 0) for dz, dc in group_zc}
+    greeted |= {(0, dx, 0, dy) for dx, dy in group_xy} | {(0, dx, dc, 0) for dx, dc in group_xc}
+    for steps in sorted(greeted, key=lambda v: (-sum(min(a, b - a) for a, b in zip(v, (NZ, NX, NC, NY))), v)):
+        pl.semaphore_signal(barrier, inc=1, device_id=device(*steps), device_id_type=MESH)
 
     tile[...] = jnp.zeros_like(tile)
     part[...] = jnp.zeros_like(part)
@@ -147,7 +151,7 @@
         info[BLOCKS : BLOCKS + 8, :] = jnp.where(c == 0, placed, pltpu.roll(placed, 2, 0))
         info_x[0] = info[...]
         return go_all(
-            1, 8, lambda j: (info, info_x.at[j], device(dx=lax.div(j, 2), dc=lax.rem(j, 2)))
+            (info, info_x.at[dx * NC + dc], device(dx=dx, dc=dc)) for dx, dc in group_xc
         )
 
     def sums(bases, into, waits=()):
@@ -223,7 +227,7 @@
 
     work(0)
     work(1)
-    pl.semaphore_wait(barrier, 7 + 12 + 14)
+    pl.semaphore_wait(barrier, len(greeted))
     give(0)
     give(1)
     arrived = count()
@@ -254,7 +258,9 @@
         whole = whole + info_x[j]
     group[...] = whole
     info_z[z] = whole
-    arrived_z = go_all(1, NZ, lambda j: (group, info_z.at[z], device(dz=j)))
+    arrived_z = go_all(
+        (group, info_z.at[z], device(dz=dz)) for dz in (4, 3, 5, 2, 6, 1, 7)
+    )
     work(5)
     give(5)
     meet(4)
@@ -305,8 +311,7 @@
     square = jnp.sum(own * own, axis=1, keepdims=True)
     sq_own[0] = as_rows([square], pad)[0:1, :]
     sq_arrived = go_all(
-        1, NX * NY,
-        lambda j: (sq_own.at[0], sq_in.at[j], device(dx=lax.div(j, NY), dy=lax.rem(j, NY))),
+        (sq_own.at[0], sq_in.at[dx * NY + dy], device(dx=dx, dy=dy)) for dx, dy in group_xy
     )
 
     arrived_z()
@@ -361,8 +366,7 @@
     inverse = lax.rsqrt(square_row / features + EPS)
     scale[mine] = inverse
     scale_arrived = go_all(
-        1, NZ * NC,
-        lambda j: (scale.at[mine], scale.at[mine], device(dz=lax.div(j, NC), dc=lax.rem(j, NC))),
+        (scale.at[mine], scale.at[mine], device(dz=dz, dc=dc)) for dz, dc in group_zc
     )
     means = own * as_columns(jnp.broadcast_to(inverse, (8, LANE)))[0:ROWS, 0:1]
 
@@ -403,11 +407,11 @@
     columns.append(jnp.concatenate([squares, jnp.zeros((ROWS - cents, 1), jnp.float32)], 0))
     final_own[...] = as_rows(columns, pad)
     final_arrived = go_all(
-        1, NX * NY,
-        lambda j: (final_own, final_in.at[j], device(dx=lax.div(j, NY), dy=lax.rem(j, NY))),
+        (final_own, final_in.at[dx * NY + dy], device(dx=dx, dy=dy)) for dx, dy in group_xy
     )
     sel_arrived = go_all(
-        1, NX, lambda j: (sel.at[pl.ds(xat(j) * per, per)], sel_in.at[x], device(dx=j))
+        (sel.at[pl.ds(pl.multiple_of(xat(dx) * per, per), per)], sel_in.at[x], device(dx=dx))
+        for dx in (2, 1, 3)
     )
     here = pl.ds(pl.multiple_of(x * per, per), per)
     sel_in[x] = sel[here, :]

time: 56.4 us -> 55.5 us (0.984)
  Pallas kernels: 55.7 us -> 54.7 us
    pallas_call x1, Pallas kernels: 53.6 us -> 52.5 us  [per_device(): pl.pallas_call(body, name='recluster', out_shape=(jax.ShapeDtypeStruct((p...]
where the time goes in v5:
time: 55.5 us; the launch traced here: 55.3 us
  Pallas kernels  54.7 us (99%)
  between operations  0.64 us (1%)
    pallas_call x1, Pallas kernels, per_device(): pl.pallas_call(body, name='recluster', out_shape=(jax.ShapeDtypeStruct((p...  52.5 us
    pallas_call x1, Pallas kernels, per_device(): pl.pallas_call(hand_out, name='hand_out', out_shape=(jax.ShapeDtypeStruct...  2.14 us

profile of v5, /device:TPU:1, one launch (start us, length us, event | category | flops | bytes accessed | tf_op | source)
XLA Modules:
  0.0 55.3 jit_solution(1283077443410176152)
XLA Ops:
  0.6 52.5 %recluster.1 = (f32[16,512]{1,0:T(8,128)}, f32[2,24]{1,0:T(2,128)}) custom-call(s32[1,4096]{1,0:T(1,128)} %bitcast.1, s32[2,24]{1,0:T(2,128)} %refs_1_.1, f32[16,512]{1,0:T(8,128)} %refs_2_.1, bf16[4096,512]{1,0:T(8,128)(2,1)} %refs_3_.1), custom_call_target="tpu_custom_call" | custom-call | tf_op jit(solution)/shard_map/recluster/pallas_call | solution.py:498
  53.2 2.1 %hand_out.1 = (f32[16,512]{1,0:T(8,128)}, f32[2,24]{1,0:T(2,128)}) custom-call(f32[16,512]{1,0:T(8,128)} %get-tuple-element.4.cent_in, f32[2,24]{1,0:T(2,128)} %get-tuple-element.5.spread_in), custom_call_target="tpu_custom_call" | custom-call | tf_op jit(solution)/shard_map/hand_out/pallas_call | solution.py:524

commit v6 on v5

--- a/solution.py
+++ b/solution.py
@@ -13,7 +13,7 @@
 ROWS = NX * OWN
 BLOCKS = NZ * NC
 LANE = 128
-ORDER = (4, 3, -3, 1, -1, 2, -2, 0)
+ORDER = (4, 3, 1, -1, -3, 2, -2, 0)
 
 
 def position(owner):
@@ -177,10 +177,13 @@
 
     cross = {}
 
-    def work(s):
-        base = zat(ORDER[s]) * (NC * ROWS)
-        bases = [base + (1 - c) * ROWS, base + c * ROWS]
-        sums(bases, [other.at[s], part.at[s]], loads if s == 0 else ())
+    def work(*slabs):
+        bases, into = [], []
+        for s in slabs:
+            base = zat(ORDER[s]) * (NC * ROWS)
+            bases += [base + (1 - c) * ROWS, base + c * ROWS]
+            into += [other.at[s], part.at[s]]
+        sums(bases, into, loads if 0 in slabs else ())
 
     def give(s):
         cross[s] = go(other.at[s], other_in.at[s], device(dc=1))
@@ -191,21 +194,26 @@
 
     xs = {}
 
+    def way_of(s):
+        return 1 if s == 1 else -1
+
     def x_start(s):
-        xs[s, 0] = go(part.at[s, xat(2)], xin.at[s, 0], device(dx=-1))
-        xs[s, 1] = go(part.at[s, xat(1)], xin.at[s, 1], device(dx=1))
+        way = way_of(s)
+        xs[s, 0] = go(part.at[s, xat(2)], xin.at[s, 0], device(dx=way))
+        xs[s, 1] = go(part.at[s, xat(-way)], xin.at[s, 1], device(dx=-way))
 
     def x_mid(s):
+        way = way_of(s)
         xs[s, 0].wait_recv()
-        part[s, xat(-1)] += xin[s, 0]
-        xs[s, 2] = go(part.at[s, xat(-1)], xin.at[s, 2], device(dx=-1))
+        part[s, xat(way)] += xin[s, 0]
+        xs[s, 2] = go(part.at[s, xat(way)], xin.at[s, 2], device(dx=way))
 
     def x_direct(s):
         for k, d in enumerate((2, 1, -1)):
             xs[s, k] = go(part.at[s, xat(d)], xin.at[s, k], device(dx=d))
 
     zs = {}
-    hops = {4: 2, 3: 1, -3: -1}
+    hops = {4: 2, 3: 1}
 
     def x_end(s):
         d = ORDER[s]
@@ -216,17 +224,17 @@
         total = part[s, x] + xin[s, 1] + xin[s, 2]
         if (s, 0) in direct:
             total = total + xin[s, 0]
-        for far in {2: (4, 3), -2: (-3,)}.get(d, ()):
+        for far in (4, 3) if d == 2 else ():
             zs[far].wait_recv()
             total = total + zin[ORDER.index(far)]
         part[s, x] = total
         if d != 0:
             zs[d] = go(part.at[s, x], zin.at[s], device(dz=hops.get(d, d)))
 
-    direct = {(s, 0) for s in (6, 7)}
-
-    work(0)
-    work(1)
+    direct = {(6, 0)}
+
+    work(0, 1)
+    scaled[...] = jnp.zeros_like(scaled)
     pl.semaphore_wait(barrier, len(greeted))
     give(0)
     give(1)
@@ -236,22 +244,27 @@
 
     def z_whole(s):
         d = ORDER[s]
-        whole_slab[s] = go(part.at[s], zslab.at[s - 3], device(dz=d))
-
-    work(2)
+        whole_slab[s] = go(part.at[s], zslab.at[s - 2], device(dz=d))
+
+    work(2, 3)
     give(2)
+    give(3)
     meet(0)
     x_start(0)
     meet(1)
     x_start(1)
-    work(3)
-    give(3)
-    meet(2)
-    x_start(2)
     work(4)
     give(4)
+    meet(2)
+    z_whole(2)
     meet(3)
     z_whole(3)
+    work(5)
+    give(5)
+    meet(4)
+    x_start(4)
+    x_mid(0)
+    x_mid(1)
     arrived()
     whole = info_x[0]
     for j in range(1, NX * NC):
@@ -261,35 +274,30 @@
     arrived_z = go_all(
         (group, info_z.at[z], device(dz=dz)) for dz in (4, 3, 5, 2, 6, 1, 7)
     )
-    work(5)
-    give(5)
-    meet(4)
-    z_whole(4)
-    x_mid(0)
-    x_mid(1)
     work(6)
     give(6)
     meet(5)
     x_start(5)
-    x_mid(2)
     work(7)
     give(7)
     meet(6)
     x_direct(6)
+    x_mid(4)
     x_end(0)
     x_end(1)
     cross[7].wait_recv()
+    whole_slab[2].wait_recv()
     whole_slab[3].wait_recv()
-    whole_slab[4].wait_recv()
     part[7] += other_in[7] + zslab[0] + zslab[1]
-    x_direct(7)
+    x_start(7)
     x_mid(5)
-    x_end(2)
+    x_end(4)
+    x_mid(7)
+    x_end(5)
     x_end(6)
-    x_end(5)
     x_end(7)
     own = part[7, x]
-    for d in (2, -2):
+    for d in (-3, 2, -2):
         zs[d].wait_recv()
         own = own + zin[ORDER.index(d)]
 
@@ -303,16 +311,16 @@
     def core_share(dz):
         at = blk(dz)
         pairs.append(go(table.at[at], table.at[at], device(dc=1)))
-
-    for dz in (2, -2, 1, -1):
-        rings[dz] = go(table.at[mine], table.at[mine], device(dz=dz))
-    core_share(0)
 
     square = jnp.sum(own * own, axis=1, keepdims=True)
     sq_own[0] = as_rows([square], pad)[0:1, :]
     sq_arrived = go_all(
         (sq_own.at[0], sq_in.at[dx * NY + dy], device(dx=dx, dy=dy)) for dx, dy in group_xy
     )
+
+    for dz in (2, -2, 1, -1):
+        rings[dz] = go(table.at[mine], table.at[mine], device(dz=dz))
+    core_share(0)
 
     arrived_z()
     total = info_z[0, 0:BLOCKS]
@@ -331,6 +339,17 @@
     for way in (1, -1):
         rings[way].wait_recv()
         core_share(-way)
+
+    sq_arrived()
+    square_row = sq_own[0]
+    for j in range(1, NX * NY):
+        square_row = square_row + sq_in[j]
+    inverse = lax.rsqrt(square_row / features + EPS)
+    scale[mine] = inverse
+    scale_arrived = go_all(
+        (scale.at[mine], scale.at[mine], device(dz=dz, dc=dc)) for dz, dc in group_zc
+    )
+    means = own * as_columns(jnp.broadcast_to(inverse, (8, LANE)))[0:ROWS, 0:1]
 
     keys_all = group[BLOCKS : BLOCKS + 8, :]
     keys = as_columns(jnp.where(c == 0, keys_all, pltpu.roll(keys_all, 6, 0)))
@@ -359,17 +378,6 @@
         [summed[first_row : first_row + ROWS], summed[first_row + ROWS : first_row + 2 * ROWS]], pad
     )
 
-    sq_arrived()
-    square_row = sq_own[0]
-    for j in range(1, NX * NY):
-        square_row = square_row + sq_in[j]
-    inverse = lax.rsqrt(square_row / features + EPS)
-    scale[mine] = inverse
-    scale_arrived = go_all(
-        (scale.at[mine], scale.at[mine], device(dz=dz, dc=dc)) for dz, dc in group_zc
-    )
-    means = own * as_columns(jnp.broadcast_to(inverse, (8, LANE)))[0:ROWS, 0:1]
-
     for way in (1, -1):
         rings[3 * way].wait_recv()
         core_share(-3 * way)
@@ -383,7 +391,6 @@
     factor = as_columns(counts[...] * scale2[...])
     for pair in pairs:
         pair.wait_recv()
-    scaled[...] = jnp.zeros_like(scaled)
     for b in range(BLOCKS):
         rows = table[b] * factor[0:ROWS, b : b + 1]
         for piece in range(3):
@@ -510,14 +517,16 @@
         ),
     )(sample_owner.reshape(1, samples), lloyd_assign, init_centroids, embeddings)
 
-    def hand_out(cent_in, spread_in, cent_out, spread_out, sem):
-        copies = [
-            pltpu.make_async_copy(cent_in, cent_out, sem.at[0]),
-            pltpu.make_async_copy(spread_in, spread_out, sem.at[1]),
-        ]
-        for copy in copies:
+    def hand_out(cent_in, spread_in, cent_out, spread_out, cent_mid, spread_mid, sem):
+        through = ((cent_in, cent_mid, cent_out), (spread_in, spread_mid, spread_out))
+        first = [pltpu.make_async_copy(v[0], v[1], sem.at[k]) for k, v in enumerate(through)]
+        last = [pltpu.make_async_copy(v[1], v[2], sem.at[2 + k]) for k, v in enumerate(through)]
+        for copy in first:
             copy.start()
-        for copy in copies:
+        for k in range(2):
+            first[k].wait()
+            last[k].start()
+        for copy in last:
             copy.wait()
 
     anywhere = pl.BlockSpec(memory_space=pl.ANY)
@@ -530,7 +539,7 @@
         ),
         in_specs=[anywhere] * 2,
         out_specs=(anywhere, anywhere),
-        scratch_shapes=[pltpu.SemaphoreType.DMA((2,))],
+        scratch_shapes=[vm((per, width), f32), vm((2, OWN), f32), pltpu.SemaphoreType.DMA((4,))],
     )(*packed)
 
 

time: 55.5 us -> 55.7 us (level)
    pallas_call x1, Pallas kernels: 52.5 us -> 53.5 us  [per_device(): pl.pallas_call(body, name='recluster', out_shape=(jax.ShapeDtypeStruct((p...]
    pallas_call x1, Pallas kernels: 2.14 us -> 1.41 us  [per_device(): pl.pallas_call(hand_out, name='hand_out', out_shape=(jax.ShapeDtypeStruct...]
where the time goes in v6:
time: 55.7 us; the launch traced here: 55.5 us
  Pallas kernels  54.9 us (99%)
  between operations  0.64 us (1%)
    pallas_call x1, Pallas kernels, per_device(): pl.pallas_call(body, name='recluster', out_shape=(jax.ShapeDtypeStruct((p...  53.5 us
    pallas_call x1, Pallas kernels, per_device(): pl.pallas_call(hand_out, name='hand_out', out_shape=(jax.ShapeDtypeStruct...  1.41 us

profile of v6, /device:TPU:1, one launch (start us, length us, event | category | flops | bytes accessed | tf_op | source)
XLA Modules:
  0.0 55.5 jit_solution(6473185765025430808)
XLA Ops:
  0.6 53.5 %recluster.1 = (f32[16,512]{1,0:T(8,128)}, f32[2,24]{1,0:T(2,128)}) custom-call(s32[1,4096]{1,0:T(1,128)} %bitcast.1, s32[2,24]{1,0:T(2,128)} %refs_1_.1, f32[16,512]{1,0:T(8,128)} %refs_2_.1, bf16[4096,512]{1,0:T(8,128)(2,1)} %refs_3_.1), custom_call_target="tpu_custom_call" | custom-call | tf_op jit(solution)/shard_map/recluster/pallas_call | solution.py:505
  54.1 1.4 %hand_out.1 = (f32[16,512]{1,0:T(8,128)}, f32[2,24]{1,0:T(2,128)}) custom-call(f32[16,512]{1,0:T(8,128)} %get-tuple-element.4.cent_in, f32[2,24]{1,0:T(2,128)} %get-tuple-element.5.spread_in), custom_call_target="tpu_custom_call" | custom-call | tf_op jit(solution)/shard_map/hand_out/pallas_call | solution.py:533

commit v7 on v6

--- a/solution.py
+++ b/solution.py
@@ -233,11 +233,9 @@
 
     direct = {(6, 0)}
 
-    work(0, 1)
-    scaled[...] = jnp.zeros_like(scaled)
+    work(0)
     pl.semaphore_wait(barrier, len(greeted))
     give(0)
-    give(1)
     arrived = count()
 
     whole_slab = {}
@@ -246,25 +244,23 @@
         d = ORDER[s]
         whole_slab[s] = go(part.at[s], zslab.at[s - 2], device(dz=d))
 
-    work(2, 3)
-    give(2)
-    give(3)
+    work(1)
+    give(1)
     meet(0)
     x_start(0)
+    work(2)
+    give(2)
     meet(1)
     x_start(1)
+    work(3)
+    give(3)
+    meet(2)
+    z_whole(2)
     work(4)
     give(4)
-    meet(2)
-    z_whole(2)
     meet(3)
     z_whole(3)
-    work(5)
-    give(5)
-    meet(4)
-    x_start(4)
     x_mid(0)
-    x_mid(1)
     arrived()
     whole = info_x[0]
     for j in range(1, NX * NC):
@@ -274,6 +270,11 @@
     arrived_z = go_all(
         (group, info_z.at[z], device(dz=dz)) for dz in (4, 3, 5, 2, 6, 1, 7)
     )
+    work(5)
+    give(5)
+    meet(4)
+    x_start(4)
+    x_mid(1)
     work(6)
     give(6)
     meet(5)
@@ -282,19 +283,19 @@
     give(7)
     meet(6)
     x_direct(6)
+    x_end(0)
     x_mid(4)
-    x_end(0)
-    x_end(1)
     cross[7].wait_recv()
     whole_slab[2].wait_recv()
     whole_slab[3].wait_recv()
     part[7] += other_in[7] + zslab[0] + zslab[1]
     x_start(7)
+    x_end(1)
     x_mid(5)
+    x_mid(7)
     x_end(4)
-    x_mid(7)
+    x_end(6)
     x_end(5)
-    x_end(6)
     x_end(7)
     own = part[7, x]
     for d in (-3, 2, -2):
@@ -327,6 +328,8 @@
     for j in range(1, NZ):
         total = total + info_z[j, 0:BLOCKS]
     counts[...] = total
+
+    scaled[...] = jnp.zeros_like(scaled)
 
     half = ROWS // 2
     for way in (1, -1):

time: 55.7 us -> 55.1 us (0.989)
  Pallas kernels: 54.9 us -> 54.3 us
    pallas_call x1, Pallas kernels: 53.5 us -> 52.8 us  [per_device(): pl.pallas_call(body, name='recluster', out_shape=(jax.ShapeDtypeStruct((p...]
where the time goes in v7:
time: 55.1 us; the launch traced here: 54.9 us
  Pallas kernels  54.3 us (99%)
  between operations  0.64 us (1%)
    pallas_call x1, Pallas kernels, per_device(): pl.pallas_call(body, name='recluster', out_shape=(jax.ShapeDtypeStruct((p...  52.8 us
    pallas_call x1, Pallas kernels, per_device(): pl.pallas_call(hand_out, name='hand_out', out_shape=(jax.ShapeDtypeStruct...  1.41 us

profile of v7, /device:TPU:1, one launch (start us, length us, event | category | flops | bytes accessed | tf_op | source)
XLA Modules:
  0.0 54.9 jit_solution(11801959472500072849)
XLA Ops:
  0.6 52.8 %recluster.1 = (f32[16,512]{1,0:T(8,128)}, f32[2,24]{1,0:T(2,128)}) custom-call(s32[1,4096]{1,0:T(1,128)} %bitcast.1, s32[2,24]{1,0:T(2,128)} %refs_1_.1, f32[16,512]{1,0:T(8,128)} %refs_2_.1, bf16[4096,512]{1,0:T(8,128)(2,1)} %refs_3_.1), custom_call_target="tpu_custom_call" | custom-call | tf_op jit(solution)/shard_map/recluster/pallas_call | solution.py:508
  53.5 1.4 %hand_out.1 = (f32[16,512]{1,0:T(8,128)}, f32[2,24]{1,0:T(2,128)}) custom-call(f32[16,512]{1,0:T(8,128)} %get-tuple-element.4.cent_in, f32[2,24]{1,0:T(2,128)} %get-tuple-element.5.spread_in), custom_call_target="tpu_custom_call" | custom-call | tf_op jit(solution)/shard_map/hand_out/pallas_call | solution.py:536

commit v8 on v7

--- a/solution.py
+++ b/solution.py
@@ -129,8 +129,6 @@
         pl.semaphore_signal(barrier, inc=1, device_id=device(*steps), device_id_type=MESH)
 
     tile[...] = jnp.zeros_like(tile)
-    part[...] = jnp.zeros_like(part)
-    other[...] = jnp.zeros_like(other)
     for load in small:
         load.wait()
     block, place = position(owner_ref[...])
@@ -154,36 +152,29 @@
             (info, info_x.at[dx * NC + dc], device(dx=dx, dc=dc)) for dx, dc in group_xc
         )
 
-    def sums(bases, into, waits=()):
-        row = lax.broadcasted_iota(jnp.int32, (ROWS, depth), 0)
-
-        def step(k):
-            at = pl.ds(pl.multiple_of(k * depth, depth), depth)
-            p = prow[:, at]
-            hot = jnp.concatenate(
-                [jnp.where(row == p - base, 1.0, 0.0).astype(jnp.bfloat16) for base in bases], 0
-            )
-            got = jnp.dot(hot, emb[at, :], preferred_element_type=jnp.float32)
-            for j, ref in enumerate(into):
-                for b in range(NX):
-                    ref[b] += got[j * ROWS : (j + 1) * ROWS, b * LANE : (b + 1) * LANE]
-
-        if waits:
-            for k in range(chunks):
-                waits[k].wait()
-                step(k)
-        else:
-            lax.fori_loop(0, chunks, lambda k, carry: (step(k), carry)[1], 0)
+    def sums(bases, into, start, size):
+        row = lax.broadcasted_iota(jnp.int32, (ROWS, size), 0)
+        p = prow[:, start : start + size]
+        hot = jnp.concatenate(
+            [jnp.where(row == p - base, 1.0, 0.0).astype(jnp.bfloat16) for base in bases], 0
+        )
+        got = jnp.dot(hot, emb[start : start + size, :], preferred_element_type=jnp.float32)
+        for j, ref in enumerate(into):
+            for b in range(NX):
+                new = got[j * ROWS : (j + 1) * ROWS, b * LANE : (b + 1) * LANE]
+                ref[b] = new if start == 0 else ref[b] + new
 
     cross = {}
 
-    def work(*slabs):
-        bases, into = [], []
-        for s in slabs:
-            base = zat(ORDER[s]) * (NC * ROWS)
-            bases += [base + (1 - c) * ROWS, base + c * ROWS]
-            into += [other.at[s], part.at[s]]
-        sums(bases, into, loads if 0 in slabs else ())
+    def work(s):
+        base = zat(ORDER[s]) * (NC * ROWS)
+        bases, into = [base + (1 - c) * ROWS, base + c * ROWS], [other.at[s], part.at[s]]
+        if s > 0:
+            sums(bases, into, 0, chunks * depth)
+            return
+        for k in range(chunks):
+            loads[k].wait()
+            sums(bases, into, k * depth, depth)
 
     def give(s):
         cross[s] = go(other.at[s], other_in.at[s], device(dc=1))
@@ -458,7 +449,7 @@
 def per_device(features, embeddings, sample_owner, lloyd_assign, init_centroids):
     samples, width = embeddings.shape
     per = init_centroids.shape[0]
-    depth = 2048
+    depth = 1024
     f32, bf16 = jnp.float32, jnp.bfloat16
     vm = pltpu.VMEM
     cents = NX * per

time: 55.1 us -> 56 us (1.016)
  Pallas kernels: 54.3 us -> 55.2 us
    pallas_call x1, Pallas kernels: 52.8 us -> 53.8 us  [per_device(): pl.pallas_call(body, name='recluster', out_shape=(jax.ShapeDtypeStruct((p...]
where the time goes in v8:
time: 56 us; the launch traced here: 55.8 us
  Pallas kernels  55.2 us (99%)
  between operations  0.64 us (1%)
    pallas_call x1, Pallas kernels, per_device(): pl.pallas_call(body, name='recluster', out_shape=(jax.ShapeDtypeStruct((p...  53.8 us
    pallas_call x1, Pallas kernels, per_device(): pl.pallas_call(hand_out, name='hand_out', out_shape=(jax.ShapeDtypeStruct...  1.41 us

profile of v8, /device:TPU:1, one launch (start us, length us, event | category | flops | bytes accessed | tf_op | source)
XLA Modules:
  0.0 55.8 jit_solution(7903894580446893077)
XLA Ops:
  0.6 53.8 %recluster.1 = (f32[16,512]{1,0:T(8,128)}, f32[2,24]{1,0:T(2,128)}) custom-call(s32[1,4096]{1,0:T(1,128)} %bitcast.1, s32[2,24]{1,0:T(2,128)} %refs_1_.1, f32[16,512]{1,0:T(8,128)} %refs_2_.1, bf16[4096,512]{1,0:T(8,128)(2,1)} %refs_3_.1), custom_call_target="tpu_custom_call" | custom-call | tf_op jit(solution)/shard_map/recluster/pallas_call | solution.py:499
  54.4 1.4 %hand_out.1 = (f32[16,512]{1,0:T(8,128)}, f32[2,24]{1,0:T(2,128)}) custom-call(f32[16,512]{1,0:T(8,128)} %get-tuple-element.4.cent_in, f32[2,24]{1,0:T(2,128)} %get-tuple-element.5.spread_in), custom_call_target="tpu_custom_call" | custom-call | tf_op jit(solution)/shard_map/hand_out/pallas_call | solution.py:527

commit v9 on v7

--- a/solution.py
+++ b/solution.py
@@ -46,7 +46,7 @@
     cent_ref, spread_ref,
     owner_ref, assign_ref, init_ref,
     emb, part, other, other_in, xin, zslab, zin,
-    prow, tile, info, info_x, group, info_z, counts, match, weight, pad, wrows,
+    prow, tile, info, info_x, both, group, info_z, counts, match, weight, pad, wrows,
     table, sq_own, sq_in, scale, scale2, scaled, final_own, final_in, sel, sel_in, lens,
     load_sem, send_sem, recv_sem,
 ):
@@ -97,7 +97,6 @@
 
         return wait
 
-    group_xc = [(dx, dc) for dx in (2, 1, 3, 0) for dc in range(NC) if (dx, dc) != (0, 0)]
     group_xy = [
         (dx, dy) for dx in (2, 1, 3, 0) for dy in (2, 1, 3, 0) if (dx, dy) != (0, 0)
     ]
@@ -124,7 +123,7 @@
     barrier = pltpu.get_barrier_semaphore()
 
     greeted = {(dz, 0, dc, 0) for dz, dc in group_zc}
-    greeted |= {(0, dx, 0, dy) for dx, dy in group_xy} | {(0, dx, dc, 0) for dx, dc in group_xc}
+    greeted |= {(0, dx, 0, dy) for dx, dy in group_xy}
     for steps in sorted(greeted, key=lambda v: (-sum(min(a, b - a) for a, b in zip(v, (NZ, NX, NC, NY))), v)):
         pl.semaphore_signal(barrier, inc=1, device_id=device(*steps), device_id_type=MESH)
 
@@ -149,10 +148,7 @@
         tile[0:2, 0:OWN] = assign_ref[...].astype(jnp.float32)
         placed = pltpu.roll(tile[...], x * OWN, 1)
         info[BLOCKS : BLOCKS + 8, :] = jnp.where(c == 0, placed, pltpu.roll(placed, 2, 0))
-        info_x[0] = info[...]
-        return go_all(
-            (info, info_x.at[dx * NC + dc], device(dx=dx, dc=dc)) for dx, dc in group_xc
-        )
+        return go(info, info_x.at[NX], device(dc=1))
 
     def sums(bases, into, waits=()):
         row = lax.broadcasted_iota(jnp.int32, (ROWS, depth), 0)
@@ -252,6 +248,9 @@
     give(2)
     meet(1)
     x_start(1)
+    arrived.wait_recv()
+    both[...] = info[...] + info_x[NX]
+    arrived = go_all((both, info_x.at[dx], device(dx=dx)) for dx in (2, 1, 3))
     work(3)
     give(3)
     meet(2)
@@ -261,15 +260,6 @@
     meet(3)
     z_whole(3)
     x_mid(0)
-    arrived()
-    whole = info_x[0]
-    for j in range(1, NX * NC):
-        whole = whole + info_x[j]
-    group[...] = whole
-    info_z[z] = whole
-    arrived_z = go_all(
-        (group, info_z.at[z], device(dz=dz)) for dz in (4, 3, 5, 2, 6, 1, 7)
-    )
     work(5)
     give(5)
     meet(4)
@@ -296,6 +286,13 @@
     x_end(4)
     x_end(6)
     x_end(5)
+    arrived()
+    whole = both[...] + info_x[1] + info_x[2] + info_x[3]
+    group[...] = whole
+    info_z[z] = whole
+    arrived_z = go_all(
+        (group, info_z.at[z], device(dz=dz)) for dz in (4, 3, 5, 2, 6, 1, 7)
+    )
     x_end(7)
     own = part[7, x]
     for d in (-3, 2, -2):
@@ -322,12 +319,6 @@
     for dz in (2, -2, 1, -1):
         rings[dz] = go(table.at[mine], table.at[mine], device(dz=dz))
     core_share(0)
-
-    arrived_z()
-    total = info_z[0, 0:BLOCKS]
-    for j in range(1, NZ):
-        total = total + info_z[j, 0:BLOCKS]
-    counts[...] = total
 
     scaled[...] = jnp.zeros_like(scaled)
 
@@ -353,6 +344,12 @@
         (scale.at[mine], scale.at[mine], device(dz=dz, dc=dc)) for dz, dc in group_zc
     )
     means = own * as_columns(jnp.broadcast_to(inverse, (8, LANE)))[0:ROWS, 0:1]
+
+    arrived_z()
+    total = info_z[0, 0:BLOCKS]
+    for j in range(1, NZ):
+        total = total + info_z[j, 0:BLOCKS]
+    counts[...] = total
 
     keys_all = group[BLOCKS : BLOCKS + 8, :]
     keys = as_columns(jnp.where(c == 0, keys_all, pltpu.roll(keys_all, 6, 0)))
@@ -452,7 +449,7 @@
         wait()
 
 
-COPIES = 7 + 7 + 8 + 18 + 2 + 5 + 8 + 8 + 15 + 15 + 15 + 3
+COPIES = 4 + 7 + 8 + 18 + 2 + 5 + 8 + 8 + 15 + 15 + 15 + 3
 
 
 def per_device(features, embeddings, sample_owner, lloyd_assign, init_centroids):
@@ -477,7 +474,8 @@
         vm((1, samples), jnp.int32),
         vm((8, LANE), f32),
         vm((24, LANE), f32),
-        vm((NX * NC, 24, LANE), f32),
+        vm((NX + 1, 24, LANE), f32),
+        vm((24, LANE), f32),
         vm((24, LANE), f32),
         vm((NZ, 24, LANE), f32),
         vm((BLOCKS, LANE), f32),

time: 55.1 us -> 56.7 us (1.029)
  Pallas kernels: 54.3 us -> 55.9 us
    pallas_call x1, Pallas kernels: 52.8 us -> 54.5 us  [per_device(): pl.pallas_call(body, name='recluster', out_shape=(jax.ShapeDtypeStruct((p...]
where the time goes in v9:
time: 56.7 us; the launch traced here: 56.5 us
  Pallas kernels  55.9 us (99%)
  between operations  0.64 us (1%)
    pallas_call x1, Pallas kernels, per_device(): pl.pallas_call(body, name='recluster', out_shape=(jax.ShapeDtypeStruct((p...  54.5 us
    pallas_call x1, Pallas kernels, per_device(): pl.pallas_call(hand_out, name='hand_out', out_shape=(jax.ShapeDtypeStruct...  1.41 us

profile of v9, /device:TPU:1, one launch (start us, length us, event | category | flops | bytes accessed | tf_op | source)
XLA Modules:
  0.0 56.5 jit_solution(8692717446667621545)
XLA Ops:
  0.6 54.5 %recluster.1 = (f32[16,512]{1,0:T(8,128)}, f32[2,24]{1,0:T(2,128)}) custom-call(s32[1,4096]{1,0:T(1,128)} %bitcast.1, s32[2,24]{1,0:T(2,128)} %refs_1_.1, f32[16,512]{1,0:T(8,128)} %refs_2_.1, bf16[4096,512]{1,0:T(8,128)(2,1)} %refs_3_.1), custom_call_target="tpu_custom_call" | custom-call | tf_op jit(solution)/shard_map/recluster/pallas_call | solution.py:506
  55.1 1.4 %hand_out.1 = (f32[16,512]{1,0:T(8,128)}, f32[2,24]{1,0:T(2,128)}) custom-call(f32[16,512]{1,0:T(8,128)} %get-tuple-element.4.cent_in, f32[2,24]{1,0:T(2,128)} %get-tuple-element.5.spread_in), custom_call_target="tpu_custom_call" | custom-call | tf_op jit(solution)/shard_map/hand_out/pallas_call | solution.py:534

commit v10 on v7

--- a/solution.py
+++ b/solution.py
@@ -508,10 +508,7 @@
     packed = pl.pallas_call(
         body,
         name="recluster",
-        out_shape=(
-            jax.ShapeDtypeStruct((per, width), f32),
-            jax.ShapeDtypeStruct((2, OWN), f32),
-        ),
+        out_shape=(vm((per, width), f32), vm((2, OWN), f32)),
         in_specs=[pl.BlockSpec(memory_space=pl.ANY)] * 4,
         out_specs=(in_vmem, in_vmem),
         scratch_shapes=scratch,
@@ -520,16 +517,14 @@
         ),
     )(sample_owner.reshape(1, samples), lloyd_assign, init_centroids, embeddings)
 
-    def hand_out(cent_in, spread_in, cent_out, spread_out, cent_mid, spread_mid, sem):
-        through = ((cent_in, cent_mid, cent_out), (spread_in, spread_mid, spread_out))
-        first = [pltpu.make_async_copy(v[0], v[1], sem.at[k]) for k, v in enumerate(through)]
-        last = [pltpu.make_async_copy(v[1], v[2], sem.at[2 + k]) for k, v in enumerate(through)]
-        for copy in first:
+    def hand_out(cent_in, spread_in, cent_out, spread_out, sem):
+        copies = [
+            pltpu.make_async_copy(cent_in, cent_out, sem.at[0]),
+            pltpu.make_async_copy(spread_in, spread_out, sem.at[1]),
+        ]
+        for copy in copies:
             copy.start()
-        for k in range(2):
-            first[k].wait()
-            last[k].start()
-        for copy in last:
+        for copy in copies:
             copy.wait()
 
     anywhere = pl.BlockSpec(memory_space=pl.ANY)
@@ -540,10 +535,10 @@
             jax.ShapeDtypeStruct((per, width), f32),
             jax.ShapeDtypeStruct((2, OWN), f32),
         ),
-        in_specs=[anywhere] * 2,
+        in_specs=[in_vmem] * 2,
         out_specs=(anywhere, anywhere),
-        scratch_shapes=[vm((per, width), f32), vm((2, OWN), f32), pltpu.SemaphoreType.DMA((4,))],
-    )(*packed)
+        scratch_shapes=[pltpu.SemaphoreType.DMA((2,))],
+    )(*(pltpu.with_memory_space_constraint(v, pltpu.VMEM) for v in packed))
 
 
 def solution(mesh):

time: 55.1 us -> 53.7 us (0.975)
  Pallas kernels: 54.3 us -> 52.9 us
    pallas_call x1, Pallas kernels: 1.41 us -> 0.64 us  [per_device(): pl.pallas_call(hand_out, name='hand_out', out_shape=(jax.ShapeDtypeStruct...]
    pallas_call x1, Pallas kernels: 52.8 us -> 52.3 us  [per_device(): pl.pallas_call(body, name='recluster', out_shape=(vm((per, width), f32),...]
where the time goes in v10:
time: 53.7 us; the launch traced here: 53.6 us
  Pallas kernels  52.9 us (99%)
  between operations  0.64 us (1%)
    pallas_call x1, Pallas kernels, per_device(): pl.pallas_call(body, name='recluster', out_shape=(vm((per, width), f32),...  52.3 us

profile of v10, /device:TPU:1, one launch (start us, length us, event | category | flops | bytes accessed | tf_op | source)
XLA Modules:
  0.0 53.6 jit_solution(12100288106270788368)
XLA Ops:
  0.6 52.3 %recluster.1 = (f32[16,512]{1,0:T(8,128)S(1)}, f32[2,24]{1,0:T(2,128)S(1)}) custom-call(s32[1,4096]{1,0:T(1,128)} %bitcast.1, s32[2,24]{1,0:T(2,128)} %refs_1_.1, f32[16,512]{1,0:T(8,128)} %refs_2_.1, bf16[4096,512]{1,0:T(8,128)(2,1)} %refs_3_.1), custom_call_target="tpu_custom_call" | custom-call | tf_op jit(solution)/shard_map/recluster/pallas_call | solution.py:508
  52.9 0.6 %hand_out.1 = (f32[16,512]{1,0:T(8,128)}, f32[2,24]{1,0:T(2,128)}) custom-call(f32[16,512]{1,0:T(8,128)S(1)} %get-tuple-element.4.cent_in, f32[2,24]{1,0:T(2,128)S(1)} %get-tuple-element.5.spread_in), custom_call_target="tpu_custom_call" | custom-call | tf_op jit(solution)/shard_map/hand_out/pallas_call | solution.py:531

commit v11 on v10

--- a/solution.py
+++ b/solution.py
@@ -154,11 +154,11 @@
             (info, info_x.at[dx * NC + dc], device(dx=dx, dc=dc)) for dx, dc in group_xc
         )
 
-    def sums(bases, into, waits=()):
-        row = lax.broadcasted_iota(jnp.int32, (ROWS, depth), 0)
+    def sums(bases, into, size, waits=()):
+        row = lax.broadcasted_iota(jnp.int32, (ROWS, size), 0)
 
         def step(k):
-            at = pl.ds(pl.multiple_of(k * depth, depth), depth)
+            at = pl.ds(pl.multiple_of(k * size, size), size)
             p = prow[:, at]
             hot = jnp.concatenate(
                 [jnp.where(row == p - base, 1.0, 0.0).astype(jnp.bfloat16) for base in bases], 0
@@ -168,12 +168,16 @@
                 for b in range(NX):
                     ref[b] += got[j * ROWS : (j + 1) * ROWS, b * LANE : (b + 1) * LANE]
 
+        def turn(k, carry):
+            step(k)
+            return carry
+
         if waits:
-            for k in range(chunks):
-                waits[k].wait()
+            for k, load in enumerate(waits):
+                load.wait()
                 step(k)
         else:
-            lax.fori_loop(0, chunks, lambda k, carry: (step(k), carry)[1], 0)
+            lax.fori_loop(0, emb.shape[0] // size, turn, 0)
 
     cross = {}
 
@@ -183,7 +187,7 @@
             base = zat(ORDER[s]) * (NC * ROWS)
             bases += [base + (1 - c) * ROWS, base + c * ROWS]
             into += [other.at[s], part.at[s]]
-        sums(bases, into, loads if 0 in slabs else ())
+        sums(bases, into, depth if 0 in slabs else 2 * depth, loads if 0 in slabs else ())
 
     def give(s):
         cross[s] = go(other.at[s], other_in.at[s], device(dc=1))
@@ -458,7 +462,7 @@
 def per_device(features, embeddings, sample_owner, lloyd_assign, init_centroids):
     samples, width = embeddings.shape
     per = init_centroids.shape[0]
-    depth = 2048
+    depth = 1024
     f32, bf16 = jnp.float32, jnp.bfloat16
     vm = pltpu.VMEM
     cents = NX * per

time: 53.7 us -> 53.5 us (level)
  no operation moved by 1% of the time
where the time goes in v11:
time: 53.5 us; the launch traced here: 53.4 us
  Pallas kernels  52.7 us (99%)
  between operations  0.64 us (1%)
    pallas_call x1, Pallas kernels, per_device(): pl.pallas_call(body, name='recluster', out_shape=(vm((per, width), f32),...  52.1 us

profile of v11, /device:TPU:1, one launch (start us, length us, event | category | flops | bytes accessed | tf_op | source)
XLA Modules:
  0.0 53.4 jit_solution(11286168228276367479)
XLA Ops:
  0.6 52.1 %recluster.1 = (f32[16,512]{1,0:T(8,128)S(1)}, f32[2,24]{1,0:T(2,128)S(1)}) custom-call(s32[1,4096]{1,0:T(1,128)} %bitcast.1, s32[2,24]{1,0:T(2,128)} %refs_1_.1, f32[16,512]{1,0:T(8,128)} %refs_2_.1, bf16[4096,512]{1,0:T(8,128)(2,1)} %refs_3_.1), custom_call_target="tpu_custom_call" | custom-call | tf_op jit(solution)/shard_map/recluster/pallas_call | solution.py:512
  52.7 0.6 %hand_out.1 = (f32[16,512]{1,0:T(8,128)}, f32[2,24]{1,0:T(2,128)}) custom-call(f32[16,512]{1,0:T(8,128)S(1)} %get-tuple-element.4.cent_in, f32[2,24]{1,0:T(2,128)S(1)} %get-tuple-element.5.spread_in), custom_call_target="tpu_custom_call" | custom-call | tf_op jit(solution)/shard_map/hand_out/pallas_call | solution.py:535
